TPU v7x, 32 devices: a whole 2x2x4 slice. The times are simulated.
32 devices in a mesh: gx: 4 (over z), gy: 4 (over y, x), gz: 2 (over core).
Axes of the slice: x: 2, y: 2, z: 4, core: 2. Of those that a mesh axis runs over, the one named last changes fastest.
Arguments:
- source: float32 [32, 128, 256], P('gx', 'gy', 'gz'), may hold values from 0.05 to 1
- target: float32 [32, 128, 256], P('gx', 'gy', 'gz'), may hold values from 0.05 to 1
- kernel_half: float32 [5], replicated, may hold values from 0.05 to 1
- smooth_half: float32 [9], replicated, may hold values from 0.1 to 1
Outputs:
- displacement: float32 [3, 32, 128, 256], P(None, 'gx', 'gy', 'gz')
- mismatch: float32 [6], replicated
All inputs are finite; a program needn't handle non-finite values.
Results may differ from a plain program's by a relative error of at most 0.0001.
Values sent between devices are 32-bit elements; how exact they have to be, the bound alone decides.
No kernel may reach another device: no remote copies, remote signals or barrier semaphores. Data moves between devices by JAX's collectives and lax.ppermute only.
A program may use at most 64 MiB of HBM per device.

v0:
```python
import functools

import jax
import jax.numpy as jnp
from jax import lax
from jax.experimental import pallas as pl
from jax.experimental.pallas import tpu as pltpu
from jax.sharding import PartitionSpec as P


ITERS = 6
LANES = 128
AXES = ("gx", "gy", "gz")


def padded_2(block, sides, width):
    for axis, dim in sides:
        count = lax.axis_size(axis)
        forward = [(i, i + 1) for i in range(count - 1)]
        backward = [(target, source) for source, target in forward]
        low = lax.ppermute(
            lax.slice_in_dim(block, block.shape[dim] - width, None, axis=dim), axis, forward
        )
        high = lax.ppermute(lax.slice_in_dim(block, 0, width, axis=dim), axis, backward)
        block = jnp.concatenate([low, block, high], axis=dim)
    return block


def full_taps(half):
    return jnp.concatenate([half[:0:-1], half])


def along(padded, taps, axis, count):
    width = taps.shape[0]
    total = taps[0] * lax.slice_in_dim(padded, 0, count, axis=axis)
    for j in range(1, width):
        total = total + taps[j] * lax.slice_in_dim(padded, j, j + count, axis=axis)
    return total


def three_passes(padded, taps, size_x, size_y, size_z):
    padded = along(padded, taps, 0, size_x)
    padded = along(padded, taps, 1, size_y)
    return along(padded, taps, 2, size_z)


def block_shards(source, target, kernel_half, smooth_half):
    kern = full_taps(kernel_half)
    radius = kernel_half.shape[0] - 1
    reach = smooth_half.shape[0] - 1
    offsets = jnp.arange(-radius, radius + 1).astype(jnp.float32)
    slope = offsets * kern
    norm_total = smooth_half[0] + 2.0 * jnp.sum(smooth_half[1:])
    smooth = full_taps(smooth_half) / norm_total
    size_x, size_y, size_z = source.shape
    cells = float(source.size * lax.axis_size("gx") * lax.axis_size("gy") * lax.axis_size("gz"))
    totals = lax.psum((jnp.sum(source), jnp.sum(target)), AXES)
    first = source * (cells / totals[0])
    second = target * (cells / totals[1])
    first_wide = padded_2(first, (("gx", 0), ("gy", 1), ("gz", 2)), radius)
    scaling_v = jnp.ones_like(source)
    errors = []
    for _ in range(ITERS):
        padded = padded_2(scaling_v, (("gx", 0), ("gy", 1), ("gz", 2)), 2 * radius)
        kv_wide = three_passes(
            padded, kern, size_x + 2 * radius, size_y + 2 * radius, size_z + 2 * radius
        )
        u_wide = first_wide / kv_wide
        ku = three_passes(u_wide, kern, size_x, size_y, size_z)
        local_err = jnp.sum(jnp.abs(scaling_v * ku - second))
        errors.append(lax.psum(local_err, AXES) / cells)
        scaling_v = second / ku
    mismatch = jnp.stack(errors)
    padded = padded_2(scaling_v, (("gx", 0), ("gy", 1), ("gz", 2)), radius)
    pass_k = along(padded, kern, 0, size_x)
    pass_g = along(padded, slope, 0, size_x)
    kk = along(pass_k, kern, 1, size_y)
    kg = along(pass_k, slope, 1, size_y)
    gk = along(pass_g, kern, 1, size_y)
    kvol = along(kk, kern, 2, size_z)
    znum = along(kk, slope, 2, size_z)
    ynum = along(kg, kern, 2, size_z)
    xnum = along(gk, kern, 2, size_z)
    raw = jnp.stack([xnum, ynum, znum]) / kvol
    padded = padded_2(raw, (("gx", 1), ("gy", 2), ("gz", 3)), reach)
    padded = along(padded, smooth, 1, size_x)
    padded = along(padded, smooth, 2, size_y)
    displacement = along(padded, smooth, 3, size_z)
    return (displacement, mismatch)


class Plan:
    def __init__(self, mesh, bx, by, bz, radius, reach):
        self.nx, self.ny, self.nc = mesh["gx"], mesh["gy"], mesh["gz"]
        self.bx, self.by, self.bz = bx, by, bz
        self.R, self.Q = radius, reach
        self.P = self.nx * self.ny
        self.X, self.Y, self.Z = bx * self.nx, by * self.ny, bz * self.nc
        self.S = self.Z // self.P
        self.H = 4 * radius
        self.gs = LANES // by if by <= LANES else 0
        self.XH = self.X // 2
        self.cells = float(self.X * self.Y * self.Z)

    def fits(self):
        return (
            self.nc == 2
            and self.ny >= 2
            and self.ny & (self.ny - 1) == 0
            and self.nx >= 2
            and self.bz == LANES
            and self.Y == LANES
            and self.gs == self.ny
            and self.bx == 2 * self.gs
            and self.Z == self.P * self.S
            and self.S == self.H
            and self.S % 8 == 0
            and self.R % 4 == 0
            and ITERS == 6
        )

    def spot(self, at):
        at %= self.P
        col, q = divmod(at, self.nx)
        return (q if col % 2 == 0 else self.nx - 1 - q), col ^ (col >> 1)

    def chip(self, at):
        i, j = self.spot(at)
        return i * self.ny + j

    def device(self, at, core):
        return self.chip(at) * self.nc + core


def swap_cores(plan, value):
    pairs = [(plan.device(at, c), plan.device(at, 1 - c)) for at in range(plan.P) for c in range(2)]
    return lax.ppermute(value, AXES, pairs)


def swap_even(plan, value):
    pairs = [(plan.device(at, c), plan.device(at ^ 1, c)) for at in range(plan.P) for c in range(2)]
    return lax.ppermute(value, AXES, pairs)


def swap_odd(plan, value):
    pairs = [
        (plan.device(at, c), plan.device(((at + 1) ^ 1) - 1, c))
        for at in range(plan.P)
        for c in range(2)
    ]
    return lax.ppermute(value, AXES, pairs)


def swap_sides(plan, value):
    pairs = [(plan.device(at, 0), plan.device(at - 1, 1)) for at in range(plan.P)]
    pairs += [(plan.device(at, 1), plan.device(at + 1, 0)) for at in range(plan.P)]
    return lax.ppermute(value, AXES, pairs)


def trade_chunks(value):
    rows, lanes = value.shape
    out = lax.all_to_all(value.reshape(rows, 1, lanes), ("gx", "gy"), 0, 0, tiled=True)
    return out.reshape(rows, lanes)


def place_of(plan):
    i, j = lax.axis_index("gx"), lax.axis_index("gy")
    at = jnp.int32(0)
    for place in range(plan.P):
        a, b = plan.spot(place)
        at = at + jnp.where((i == a) & (j == b), place, 0)
    return at.astype(jnp.int32)


def call(kernel, out_shape, n_smem, n_vmem, scratch=(), smem_out=0, n_any=0, any_out=0, aliases=None):
    vm, sm = pl.BlockSpec(memory_space=pltpu.VMEM), pl.BlockSpec(memory_space=pltpu.SMEM)
    hbm = pl.BlockSpec(memory_space=pltpu.HBM)
    out_specs = [vm] * (len(out_shape) - smem_out - any_out) + [sm] * smem_out + [hbm] * any_out
    return pl.pallas_call(
        kernel,
        out_shape=out_shape,
        in_specs=[sm] * n_smem + [vm] * n_vmem + [hbm] * n_any,
        out_specs=out_specs,
        scratch_shapes=list(scratch),
        input_output_aliases=aliases or {},
        compiler_params=pltpu.CompilerParams(vmem_limit_bytes=48 << 20),
    )


def f32(*shape):
    return jax.ShapeDtypeStruct(shape, jnp.float32)


def turn_groups(plan, parts):
    n, w = plan.gs, plan.by
    group = lax.broadcasted_iota(jnp.int32, parts[0].shape, 1) // w
    outs = []
    for a in range(n):
        total = parts[a]
        for b in range(n):
            if b != a:
                moved = pltpu.roll(parts[b], (w * (b - a)) % LANES, 1)
                total = jnp.where(group == b, moved, total)
        outs.append(total)
    return outs


def pack_kernel(plan, src_hbm, tgt_hbm, keep_ref, stat_ref, src_ref, tgt_ref, sems):
    c = lax.axis_index("gz")
    copies = [
        pltpu.make_async_copy(src_hbm, src_ref, sems.at[0]),
        pltpu.make_async_copy(tgt_hbm, tgt_ref, sems.at[1]),
    ]
    for copy in copies:
        copy.start()
    sums = []
    for st, ref in enumerate((src_ref, tgt_ref)):
        copies[st].wait()
        keep_ref[st] = ref[pl.ds(plan.gs * c, plan.gs)].reshape(LANES, LANES).T
        row = jnp.sum(ref[...].reshape(plan.bx * plan.by, LANES), axis=0, keepdims=True)
        sums.append(row + pltpu.roll(row, LANES // 2, 1))
    stat_ref[...] = jnp.where(lane_at() < LANES // 2, *sums)


def lane_at():
    return lax.broadcasted_iota(jnp.int32, (1, LANES), 1)


def chunk_kernel(plan, keep_ref, src_ref, tgt_ref, stat_ref, out_ref, recv_ref):
    c = lax.axis_index("gz")
    half, S = plan.P // 2, plan.S
    size = 2 * S + 1
    for st, ref in enumerate((src_ref, tgt_ref)):
        recv_ref[st] = ref[pl.ds(plan.gs * c, plan.gs)].reshape(LANES, LANES).T

    def write(low_ref, high_ref):
        stat = stat_ref[...]
        for place in range(plan.P):
            ref, part = (low_ref, place) if place < half else (high_ref, place - half)
            base = size * plan.chip(place)
            for st in range(2):
                out_ref[base + S * st : base + S * st + S, :] = ref[st, S * part : S * part + S, :]
            out_ref[base + 2 * S : base + size, :] = stat

    pl.when(c == 0)(lambda: write(keep_ref, recv_ref))
    pl.when(c == 1)(lambda: write(recv_ref, keep_ref))


def unpack_kernel(plan, in_ref, s_ref, t_ref):
    S, gs, XH = plan.S, plan.gs, plan.XH
    size = 2 * S + 1
    for st, out_ref in enumerate((s_ref, t_ref)):
        for i in range(plan.nx):
            bases = [size * (i * plan.ny + j) + S * st for j in range(plan.ny)]
            parts = [in_ref[base : base + S, :] for base in bases]
            for xx, value in enumerate(turn_groups(plan, parts)):
                out_ref[i * gs + xx] = value
    t_ref[XH] = jnp.zeros((S, LANES), jnp.float32)
    t_ref[XH, :1, :] = sum_rows(plan, in_ref, size)


def sum_rows(plan, ref, size):
    total = ref[size - 1 : size, :]
    for p in range(1, plan.P):
        total = total + ref[size * p + size - 1 : size * p + size, :]
    return total


def banded(taps, n, odd):
    row = lax.broadcasted_iota(jnp.int32, (n, n), 0)
    col = lax.broadcasted_iota(jnp.int32, (n, n), 1)
    gap = row - col
    total = jnp.zeros((n, n), jnp.float32)
    for d, tap in enumerate(taps):
        if odd:
            if d:
                total = jnp.where(gap == d, d * tap, total)
                total = jnp.where(gap == -d, -(d * tap), total)
        else:
            total = jnp.where(jnp.abs(gap) == d, tap, total)
    return total


def halves(value):
    high = value.astype(jnp.bfloat16)
    return high, (value - high.astype(jnp.float32)).astype(jnp.bfloat16)


def quad(matrix):
    high, low = halves(matrix)
    row = jnp.concatenate([high, low], axis=1)
    return jnp.concatenate([row, row], axis=0)


def lanes_times(value, quad_ref):
    high, low = halves(value)
    both = jnp.concatenate([high, low], axis=1)
    out = jnp.dot(both, quad_ref[...], preferred_element_type=jnp.float32)
    return out[:, :LANES] + out[:, LANES:]


def even_sum(load, taps, mid):
    total = taps[0] * load(mid)
    for d in range(1, len(taps)):
        total = total + taps[d] * (load(mid - d) + load(mid + d))
    return total


def unit_sum(load, taps, mid):
    total = load(mid)
    for d in range(1, len(taps)):
        total = total + taps[d] * (load(mid - d) + load(mid + d))
    return total


def odd_sum(load, taps, mid):
    total = taps[1] * (load(mid + 1) - load(mid - 1))
    for d in range(2, len(taps)):
        total = total + (d * taps[d]) * (load(mid + d) - load(mid - d))
    return total


MANY = 8


def run_passes(plan, passes):
    chunks = range(0, plan.X, MANY)
    for base in chunks:
        passes[0][0](base)
    for (_, matmul_part, emit_part), after in zip(passes, passes[1:] + [None]):
        done = None

        def close(pair):
            emit_part(*pair)
            if after is not None:
                after[0](pair[0])

        for base in chunks:
            out = matmul_part(base)
            if done is not None:
                close(done)
            done = (base, out)
        close(done)


def kernel_pass(plan, taps, quad_ref, in_ref, zb_ref, rows, emit):
    R = plan.R

    def z_part(base):
        for x in range(base, base + MANY):
            zb_ref[R + x, :rows, :] = unit_sum(lambda j: in_ref[x, j : j + rows, :], taps, R)

    def matmul_part(base):
        parts = [
            unit_sum(lambda j: zb_ref[base + q + j, :rows, :], taps, R) for q in range(MANY)
        ]
        return lanes_times(jnp.concatenate(parts, axis=0), quad_ref)

    def emit_part(base, out):
        for q in range(MANY):
            emit(base + q, out[q * rows : (q + 1) * rows])

    return z_part, matmul_part, emit_part


def inside(plan, at, off, rows):
    z = lax.broadcasted_iota(jnp.int32, (rows, LANES), 0) + (at * plan.S - plan.H + off)
    return (z >= 0) & (z < plan.Z)


def scale_step(plan, at, taps, quad_ref, zb, src, top, dst, over, off, start, rows):
    mask = inside(plan, at, off + start, rows)
    src = src.at[:, pl.ds(top, rows + 2 * plan.R), :]
    lead = (off + 7) // 8 * 8
    over = over.at[:, pl.ds(start, rows + lead), :]

    def emit(x, value):
        dst[x, pl.ds(start, rows), :] = jnp.where(mask, over[x, off : off + rows, :] / value, 0.0)

    return kernel_pass(plan, taps, quad_ref, src, zb, rows, emit)


def clear_edges(ref, edge, size):
    blank = jnp.zeros((edge,) + ref.shape[1:], jnp.float32)
    ref[:edge] = blank
    ref[edge + size :] = blank


def prep_kernel(plan, k_ref, s_ref, own, taps_ref, quad_ref, slope_ref, smooth_ref, high_ref, low_ref):
    del own
    R, Q = plan.R, plan.Q
    taps = [jnp.zeros((1, LANES), jnp.float32) + k_ref[d] for d in range(R + 1)]
    taps = [jnp.ones((1, LANES), jnp.float32)] + [tap / taps[0] for tap in taps[1:]]
    stap = smooth_taps(s_ref, Q)
    for d in range(R + 1):
        taps_ref[d] = jnp.broadcast_to(taps[d], (8, LANES))
    for d in range(Q + 1):
        taps_ref[R + 1 + d] = jnp.broadcast_to(stap[d], (8, LANES))
    quad_ref[...] = quad(banded(taps, LANES, False))
    slope_ref[...] = quad(banded(taps, LANES, True))
    smooth_ref[...] = quad(banded(stap, LANES, False))
    wide = [jnp.concatenate([t] * (plan.Z // LANES), axis=1) for t in stap]
    high_ref[...], low_ref[...] = halves(banded(wide, plan.Z, False))


def kernel_taps(plan, taps_ref):
    return [taps_ref[d, :1, :] for d in range(plan.R + 1)]


def gaps_of(plan, tot, tw, olds, news):
    S = plan.S
    first_half = lane_at() < LANES // 2
    both = tot[:1, :]
    sum_s = jnp.sum(jnp.where(first_half, both, 0.0), axis=1, keepdims=True)
    sum_t = jnp.sum(jnp.where(first_half, 0.0, both), axis=1, keepdims=True)
    scale_s = plan.cells / jnp.broadcast_to(sum_s, (1, LANES))
    scale_t = plan.cells / jnp.broadcast_to(sum_t, (1, LANES))

    def mid(ref, x):
        edge = (ref.shape[1] - S) // 2
        return ref[x, edge : edge + S, :]

    def p_step(x, carry):
        t = mid(tw, x)
        want = scale_t * t
        have = scale_s * t
        result = []
        for part, old, new in zip(carry, olds, news):
            value = have / mid(new, x)
            if old is not None:
                value = value * mid(old, x)
            gap = jnp.abs(value - want)
            for r in range(0, S, 8):
                part = part + gap[r : r + 8]
            result.append(part)
        return tuple(result)

    zero = jnp.zeros((8, LANES), jnp.float32)
    gaps = lax.fori_loop(0, plan.X, p_step, (zero,) * len(news), unroll=4)
    return [jnp.sum(g, keepdims=True) for g in gaps]


def in_lanes(values, first=0):
    row = jnp.zeros((1, LANES), jnp.float32)
    for t, value in enumerate(values):
        row = jnp.where(lane_at() == first + t, value, row)
    return row


def gaps_kernel(plan, tot, tw, v1, v2, v3, v4, out_ref):
    out_ref[...] = in_lanes(gaps_of(plan, tot, tw, (None, v1, v2, v3), (v1, v2, v3, v4)))


def spread_halves(plan, at, own, even, odd, own2, even2, odd2, win):
    S, H, gs = plan.S, plan.H, plan.gs
    c = lax.axis_index("gz")

    def spread(low, high):
        for k, (mid, core) in enumerate(((own, c), (own2, 1 - c))):
            for i in range(plan.nx):
                x, here = plan.bx * i + gs * core, pl.ds(i * gs, gs)
                win[pl.ds(x, gs), H : H + S, :] = mid[here]
                win[pl.ds(x, gs), :H, :] = low[k][here]
                win[pl.ds(x, gs), H + S :, :] = high[k][here]

    pl.when(at % 2 == 0)(lambda: spread((odd, odd2), (even, even2)))
    pl.when(at % 2 == 1)(lambda: spread((even, even2), (odd, odd2)))


def open_kernel(plan, taps_ref, quad_ref, own, even, odd, own2, even2, odd2, sw, ku, u, zb):
    R, S, H, X = plan.R, plan.S, plan.H, plan.X
    at = place_of(plan)
    taps = kernel_taps(plan, taps_ref)
    clear_edges(zb, R, X)
    spread_halves(plan, at, own, even, odd, own2, even2, odd2, sw)

    def reach_sum(place, size):
        total = jnp.ones(place.shape, jnp.float32)
        for d in range(1, R + 1):
            total = total + jnp.where(place - d >= 0, taps[d], 0.0)
            total = total + jnp.where(place + d < size, taps[d], 0.0)
        return total

    rows = S + 2 * H
    mask = inside(plan, at, 0, rows)
    y_at = lax.broadcasted_iota(jnp.int32, (rows, LANES), 1)
    z_at = lax.broadcasted_iota(jnp.int32, (rows, LANES), 0) + (at * S - H)
    plane = reach_sum(z_at, plan.Z) * (reach_sum(y_at, plan.Y) * taps_ref[0, :1, :])

    def u_step(x, carry):
        cx = reach_sum(jnp.zeros((1, LANES), jnp.int32) + x, X)
        u[x] = jnp.where(mask, sw[x] / (plane * cx), 0.0)
        return carry

    lax.fori_loop(0, X, u_step, 0, unroll=2)

    def emit(x, value):
        ku[x] = value

    run_passes(plan, [kernel_pass(plan, taps, quad_ref, u, zb, rows - 2 * R, emit)])


def first_kernel(plan, taps_ref, quad_ref, own, even, odd, own2, even2, odd2, sw, ku,
                 tw, v, v2, u_out, tot, u, zb, zc):
    R, S, H, X, XH = plan.R, plan.S, plan.H, plan.X, plan.XH
    at = place_of(plan)
    taps = kernel_taps(plan, taps_ref)
    clear_edges(zb, R, X)
    clear_edges(zc, R, X)
    spread_halves(plan, at, own, even, odd, own2, even2, odd2, tw)
    tot[...] = own[XH, :1, :] + own2[XH, :1, :]
    rows = S + 2 * H - 2 * R
    mask = inside(plan, at, R, rows)

    def v_step(x, carry):
        v[x] = jnp.where(mask, tw[x, R : R + rows, :] / ku[x], 0.0)
        return carry

    lax.fori_loop(0, X, v_step, 0, unroll=4)
    step = functools.partial(scale_step, plan, at, taps, quad_ref)
    run_passes(plan, [
        step(zb, v, 0, u, sw, 2 * R, 0, rows - 2 * R),
        step(zc, u, 0, v2, tw, 3 * R, 0, rows - 4 * R),
        step(zb, v2, 0, u_out, sw, 4 * R, 0, rows - 6 * R),
    ])


def early_kernel(plan, taps_ref, quad_ref, mine, side, sw, tw, v, u, v2, win, zb, zc):
    R, S, H = plan.R, plan.S, plan.H
    c = lax.axis_index("gz")
    at = place_of(plan)
    taps = kernel_taps(plan, taps_ref)
    clear_edges(zb, R, plan.X)
    clear_edges(zc, R, plan.X)
    real = jnp.where(jnp.where(c == 0, at > 0, at < plan.P - 1), 1.0, 0.0)
    win[:, pl.ds(pl.multiple_of(H * c, 8), H), :] = side[...] * real
    win[:, pl.ds(pl.multiple_of(H * (1 - c), 8), S), :] = mine[...]
    step = functools.partial(scale_step, plan, at, taps, quad_ref)
    from_ = pl.multiple_of(S * c, 8)
    run_passes(plan, [
        step(zb, win, 0, v, tw, R, from_, S + H - 2 * R),
        step(zc, v, from_, u, sw, 2 * R, from_, S + H - 4 * R),
        step(zb, u, from_, v2, tw, 3 * R, from_, S + H - 6 * R),
    ])


def late_rows(plan, at, taps, quad_ref, mine, other, sw, tw, v, u, v2, win, zb, zc):
    R, S, H = plan.R, plan.S, plan.H
    c = lax.axis_index("gz")
    real = jnp.where(jnp.where(c == 1, at > 0, at < plan.P - 1), 1.0, 0.0)
    half = S // 2

    def lay(other_at, mine_at, mine_from):
        win[:, other_at : other_at + H, :] = other[...] * real
        win[:, mine_at : mine_at + half, :] = mine[:, mine_from : mine_from + half, :]

    pl.when(c == 0)(lambda: lay(half, 0, half))
    pl.when(c == 1)(lambda: lay(0, H, 0))
    step = functools.partial(scale_step, plan, at, taps, quad_ref)
    first = pl.multiple_of((S + H - 2 * R) * (1 - c), 8)
    second = pl.multiple_of((S + H - 4 * R) * (1 - c), 8)
    third = pl.multiple_of((S + H - 6 * R) * (1 - c), 8)
    return [
        step(zb, win, 0, v, tw, R, first, S),
        step(zc, v, second, u, sw, 2 * R, second, S),
        step(zb, u, third, v2, tw, 3 * R, third, S),
    ]


def late_kernel(plan, taps_ref, quad_ref, mine, other, sw, tw, v_in, u_in, v2_in,
                v, u, v2, u_out, win, zb, zc):
    del v_in, u_in, v2_in
    R, S = plan.R, plan.S
    at = place_of(plan)
    taps = kernel_taps(plan, taps_ref)
    clear_edges(zb, R, plan.X)
    clear_edges(zc, R, plan.X)
    passes = late_rows(plan, at, taps, quad_ref, mine, other, sw, tw, v, u, v2, win, zb, zc)
    passes.append(scale_step(plan, at, taps, quad_ref, zc, v2, 0, u_out, sw, 4 * R, 0, S))
    run_passes(plan, passes)


def smooth_taps(s_ref, reach):
    total = s_ref[0]
    tail = s_ref[1]
    for d in range(2, reach + 1):
        tail = tail + s_ref[d]
    scale = 1.0 / (jnp.zeros((1, LANES), jnp.float32) + (total + 2.0 * tail))
    return [scale * s_ref[d] for d in range(reach + 1)]


def last_kernel(plan, taps_ref, quad_ref, slope_ref, smooth_ref, mine, other, sw, tw, prev,
                gaps, tot, v_in, u_in, v2_in, v, u, v2, out_ref, win, zb, zc, zg, raw):
    del v_in, u_in, v2_in
    R, S, X, gs, Q = plan.R, plan.S, plan.X, plan.gs, plan.Q
    size = 3 * S + 1
    c = lax.axis_index("gz")
    at = place_of(plan)
    taps = kernel_taps(plan, taps_ref)
    stap = [taps_ref[R + 1 + d, :1, :] for d in range(Q + 1)]
    clear_edges(zb, R, X)
    clear_edges(zc, R, X)
    clear_edges(zg, R, X)
    for comp in range(3):
        clear_edges(raw.at[comp], Q, X)
    passes = late_rows(plan, at, taps, quad_ref, mine, other, sw, tw, v, u, v2, win, zb, zc)

    def z_part(base):
        for x in range(base, base + MANY):
            load = lambda j: v2[x, j : j + S, :]
            zc[R + x, :S, :] = unit_sum(load, taps, R)
            zg[R + x, :S, :] = odd_sum(load, taps, R)

    def matmul_part(base):
        kk, gk, kg = [], [], []
        for q in range(MANY):
            flat = lambda j: zc[base + q + j, :S, :]
            kk.append(unit_sum(flat, taps, R))
            gk.append(odd_sum(flat, taps, R))
            kg.append(unit_sum(lambda j: zg[base + q + j, :S, :], taps, R))
        kk, gk, kg = (jnp.concatenate(part, axis=0) for part in (kk, gk, kg))
        nums = lanes_times(gk, quad_ref), lanes_times(kk, slope_ref), lanes_times(kg, quad_ref)
        return lanes_times(kk, quad_ref), nums

    def emit_part(base, out):
        kvol, nums = out
        for comp, num in enumerate(nums):
            value = num / kvol
            for q in range(MANY):
                raw[comp, Q + base + q] = value[q * S : (q + 1) * S]

    run_passes(plan, passes + [(z_part, matmul_part, emit_part)])

    for i in range(plan.nx):
        x = plan.bx * i + gs * c
        for comp in range(3):
            parts = []
            for xx in range(gs):
                parts.append(even_sum(lambda j: raw[comp, x + xx + j], stap, Q))
            flat = lanes_times(jnp.concatenate(parts, axis=0), smooth_ref)
            turned = turn_groups(plan, [flat[xx * S : (xx + 1) * S] for xx in range(gs)])
            for j in range(plan.ny):
                base = size * (i * plan.ny + j) + comp * S
                out_ref[base : base + S, :] = turned[j]

    rows = gaps_of(plan, tot, tw, (prev, v), (v, v2))
    stat = gaps[...] + in_lanes(rows, ITERS - 2)
    for p in range(plan.P):
        out_ref[size * p + 3 * S : size * (p + 1), :] = stat


def smooth_z(plan, core, high_ref, low_ref, in_ref, data, emit):
    S = plan.S
    size = 3 * S + 1
    for place in range(plan.P):
        for comp in range(3):
            base = size * plan.chip(place) + comp * S
            data[S * place : S * place + S, comp * LANES : (comp + 1) * LANES] = in_ref[
                base : base + S, :
            ]
    rows = pl.ds(pl.multiple_of(core * LANES, LANES), LANES)
    m_high, m_low = high_ref[rows, :], low_ref[rows, :]
    d_high, d_low = halves(data[...])
    dot = functools.partial(jnp.dot, preferred_element_type=jnp.float32)
    out = dot(m_high, d_high) + (dot(m_high, d_low) + dot(m_low, d_high))
    for comp in range(3):
        emit(comp, out[:, comp * LANES : (comp + 1) * LANES].T)


def away_kernel(plan, high_ref, low_ref, in_ref, send_ref, data):
    def emit(comp, value):
        send_ref[comp] = value

    smooth_z(plan, 1 - lax.axis_index("gz"), high_ref, low_ref, in_ref, data, emit)


def home_kernel(plan, high_ref, low_ref, in_ref, mis_ref, out_hbm, data, keep, sem):
    c = lax.axis_index("gz")
    gs = plan.gs

    def emit(comp, value):
        keep[comp] = value.reshape(gs, plan.by, LANES)

    smooth_z(plan, c, high_ref, low_ref, in_ref, data, emit)
    copy = pltpu.make_async_copy(keep, out_hbm.at[:, pl.ds(gs * c, gs)], sem)
    copy.start()
    gone = sum_rows(plan, in_ref, 3 * plan.S + 1) / plan.cells
    for t in range(ITERS):
        mis_ref[t] = jnp.sum(jnp.where(lane_at() == t, gone, 0.0))
    copy.wait()


def place_kernel(plan, recv_ref, in_hbm, out_hbm, sem):
    del in_hbm
    c = lax.axis_index("gz")
    copy = pltpu.make_async_copy(recv_ref, out_hbm.at[:, pl.ds(plan.gs * (1 - c), plan.gs)], sem)
    copy.start()
    copy.wait()


def slab_shards(plan, source, target, kernel_half, smooth_half):
    R, S, H, X, XH, Pn, Z = plan.R, plan.S, plan.H, plan.X, plan.XH, plan.P, plan.Z
    bind = lambda kernel: functools.partial(kernel, plan)
    half = f32(2, LANES, LANES)
    vm = lambda *shape: pltpu.VMEM(shape, jnp.float32)
    keep, stat = call(
        bind(pack_kernel), [half, f32(1, LANES)], 0, 0,
        [vm(*source.shape), vm(*source.shape), pltpu.SemaphoreType.DMA((2,))], n_any=2,
    )(*(pltpu.with_memory_space_constraint(a, pltpu.HBM) for a in (source, target)))
    (chunks,) = call(
        bind(chunk_kernel), [f32(Pn * (2 * S + 1), LANES)], 0, 4, [vm(*half.shape)]
    )(keep, swap_cores(plan, source), swap_cores(plan, target), stat)
    spread = trade_chunks(chunks)
    own_s, own_t = call(
        bind(unpack_kernel), [f32(XH, S, LANES), f32(XH + 1, S, LANES)], 0, 1
    )(spread)
    square = jax.ShapeDtypeStruct((2 * LANES, 2 * LANES), jnp.bfloat16)
    table = jax.ShapeDtypeStruct((Z, Z), jnp.bfloat16)
    taps, quad_k, quad_g, quad_s, high, low = call(
        bind(prep_kernel), [f32(plan.R + plan.Q + 2, 8, LANES), square, square, square, table, table],
        2, 0, n_any=1,
    )(kernel_half, smooth_half, own_s)
    even_s, odd_s = swap_even(plan, own_s), swap_odd(plan, own_s)
    even_t, odd_t = swap_even(plan, own_t), swap_odd(plan, own_t)
    own2_s, own2_t = swap_cores(plan, own_s), swap_cores(plan, own_t)
    even_s, odd_s, taps = lax.optimization_barrier((even_s, odd_s, taps))
    halos_s = swap_cores(plan, even_s), swap_cores(plan, odd_s)
    even_t, odd_t, own2_s = lax.optimization_barrier((even_t, odd_t, own2_s))
    halos_t = swap_cores(plan, even_t), swap_cores(plan, odd_t)

    slab = f32(X, S, LANES)
    width = S + 2 * H
    wide, v_shape, u_shape, v2_shape = (f32(X, width - 2 * k * R, LANES) for k in (0, 1, 2, 3))
    zb = vm(X + 2 * R, width - 2 * R, LANES)
    sw, ku = call(
        bind(open_kernel), [wide, v_shape], 0, 8, [vm(*wide.shape), zb]
    )(taps, quad_k, own_s, even_s, odd_s, own2_s, *halos_s)
    tw, v1, v2, u, tot = call(
        bind(first_kernel), [wide, v_shape, v2_shape, slab, f32(1, LANES)], 0, 10,
        [vm(*u_shape.shape), zb, zb],
    )(taps, quad_k, own_t, even_t, odd_t, own2_t, *halos_t, sw, ku)

    def early(u, side):
        return call(
            bind(early_kernel), [v_shape, u_shape, v2_shape], 0, 6,
            [vm(X, S + H, LANES), zb, zb],
        )(taps, quad_k, u, side, sw, tw)

    rest = vm(X, H + S // 2, LANES)
    side = swap_sides(plan, u)
    other = swap_cores(plan, side)
    v3, u4, v4 = early(u, side)
    v3, _, v4, u = call(
        bind(late_kernel), [v_shape, u_shape, v2_shape, slab], 0, 9, [rest, zb, zb],
        aliases={6: 0, 7: 1, 8: 2},
    )(taps, quad_k, u, other, sw, tw, v3, u4, v4)
    side = swap_sides(plan, u)
    (gaps,) = call(bind(gaps_kernel), [f32(1, LANES)], 0, 6)(tot, tw, v1, v2, v3, v4)
    side, gaps = lax.optimization_barrier((side, gaps))
    other = swap_cores(plan, side)
    v5, u6, v6 = early(u, side)
    *_, chunks = call(
        bind(last_kernel), [v_shape, u_shape, v2_shape, f32(Pn * (3 * S + 1), LANES)], 0, 14,
        [rest, zb, zb, vm(X + 2 * R, S, LANES), vm(3, X + 2 * plan.Q, S, LANES)],
        aliases={11: 0, 12: 1, 13: 2},
    )(taps, quad_k, quad_g, quad_s, u, other, sw, tw, v4, gaps, tot, v5, u6, v6)
    spread = trade_chunks(chunks)
    data = vm(Z, 3 * LANES)
    (send,) = call(bind(away_kernel), [f32(3, LANES, LANES)], 0, 3, [data])(high, low, spread)
    half = (3, plan.gs, plan.by, LANES)
    recv = swap_cores(plan, send.reshape(half))
    whole = f32(3, plan.bx, plan.by, LANES)
    mismatch, displacement = call(
        bind(home_kernel), [f32(ITERS), whole], 0, 3, [data, vm(*half), pltpu.SemaphoreType.DMA(())],
        smem_out=1, any_out=1,
    )(high, low, spread)
    (displacement,) = call(
        bind(place_kernel), [whole], 0, 1, [pltpu.SemaphoreType.DMA(())], n_any=1, any_out=1,
        aliases={1: 0},
    )(recv, displacement)
    return displacement, mismatch


def shards(sizes, source, target, kernel_half, smooth_half):
    plan = Plan(sizes, *source.shape, kernel_half.shape[0] - 1, smooth_half.shape[0] - 1)
    if plan.fits():
        return slab_shards(plan, source, target, kernel_half, smooth_half)
    return block_shards(source, target, kernel_half, smooth_half)


def solution(mesh):
    in_specs = (P("gx", "gy", "gz"), P("gx", "gy", "gz"), P(), P())
    out_specs = (P(None, "gx", "gy", "gz"), P())
    body = functools.partial(shards, dict(mesh.shape))
    return jax.shard_map(body, mesh=mesh, in_specs=in_specs, out_specs=out_specs, check_vma=False)
```

profile of v0, /device:TPU:0, one launch (start us, length us, event | category | flops | bytes accessed | tf_op | source)
XLA Modules:
  0.0 74.5 jit_solution(7760618661108586993)
XLA Ops:
  0.6 0.6 collective-permute-start
  1.2 0.1 collective-permute-start.1
  1.3 1.2 %shard_map.59 = (f32[2,128,128]{2,1,0:T(8,128)S(1)}, f32[1,128]{1,0:T(1,128)S(1)}) custom-call(f32[8,32,128]{2,1,0:T(8,128)} %src_hbm.1, f32[8,32,128]{2,1,0:T(8,128)} %tgt_hbm.1), custom_call_target="tpu_custom_call" | custom-call | tf_op jit(solution)/shard_map/pallas_call | solution.py:706
  2.5 0.0 collective-permute-done.src_ref
  2.5 0.3 collective-permute-done.1.tgt_ref
  2.7 0.1 shard_map.60
  2.9 18.4 %all_to_all.10 = f32[528,1,128]{2,1,0:T(1,128)S(1)} all-to-all(f32[528,1,128]{2,1,0:T(1,128)S(1)} %bitcast.11), channel_id=1, replica_groups=mesh['gx'=4,'gy'=4,'gz'=2] {'gx','gy'}, dimensions={0} | all-to-all | bytes 540672 | tf_op jit(solution)/shard_map/all_to_all | solution.py:162
  21.2 0.3 shard_map.61
  21.5 0.0 copy-start
  21.5 0.0 copy-start.1
  21.5 1.0 %collective-permute-start.5 = (f32[17,16,128]{2,1,0:T(8,128)S(1)}, f32[17,16,128]{2,1,0:T(8,128)S(1)}, u32[]{:S(2)}, u32[]{:S(2)}) collective-permute-start(f32[17,16,128]{2,1,0:T(8,128)S(1)} %get-tuple-element.49.own), channel_id=1, source_target_pairs={{0,4},{1,5},{8,16},{9,17},{16,8},{17,9},{24,26},{25,27},{26,24},{2... | collective-permute-start | bytes 417800 | tf_op jit(solution)/shard_map/ppermute | solution.py:151
  22.5 0.3 collective-permute-start.4
  22.8 0.0 collective-permute-start.6
  22.8 1.0 %collective-permute-start.3 = (f32[16,16,128]{2,1,0:T(8,128)S(1)}, f32[16,16,128]{2,1,0:T(8,128)S(1)}, u32[]{:S(2)}, u32[]{:S(2)}) collective-permute-start(f32[16,16,128]{2,1,0:T(8,128)S(1)} %get-tuple-element.41.own), channel_id=1, source_target_pairs={{0,4},{1,5},{8,16},{9,17},{16,8},{17,9},{24,26},{25,27},{26,24},{2... | collective-permute-start | bytes 393224 | tf_op jit(solution)/shard_map/ppermute | solution.py:151
  23.8 1.2 %collective-permute-start.2 = (f32[16,16,128]{2,1,0:T(8,128)S(1)}, f32[16,16,128]{2,1,0:T(8,128)S(1)}, u32[]{:S(2)}, u32[]{:S(2)}) collective-permute-start(f32[16,16,128]{2,1,0:T(8,128)S(1)} %get-tuple-element.41.own), channel_id=1, source_target_pairs={{0,8},{1,9},{8,0},{9,1},{16,24},{17,25},{24,16},{25,17},{26,18},{2... | collective-permute-start | bytes 393224 | tf_op jit(solution)/shard_map/ppermute | solution.py:142
  25.0 0.0 collective-permute-done.6.own2
  25.0 0.0 collective-permute-start.7
  25.0 2.4 %collective-permute-done.5.odd = f32[17,16,128]{2,1,0:T(8,128)S(1)} collective-permute-done((f32[17,16,128]{2,1,0:T(8,128)S(1)}, f32[17,16,128]{2,1,0:T(8,128)S(1)}, u32[]{:S(2)}, u32[]{:S(2)}) %collective-permute-start.5) | collective-permute-done | bytes 139296 | tf_op jit(solution)/shard_map/ppermute | solution.py:151
  27.4 1.1 %collective-permute-done.4.even = f32[17,16,128]{2,1,0:T(8,128)S(1)} collective-permute-done((f32[17,16,128]{2,1,0:T(8,128)S(1)}, f32[17,16,128]{2,1,0:T(8,128)S(1)}, u32[]{:S(2)}, u32[]{:S(2)}) %collective-permute-start.4) | collective-permute-done | bytes 139296 | tf_op jit(solution)/shard_map/ppermute | solution.py:142
  28.5 0.0 collective-permute-start.8
  28.5 0.5 collective-permute-start.9
  29.0 0.0 copy-done
  29.0 0.0 copy-done.1
  29.0 0.8 %shard_map.62 = (f32[14,8,128]{2,1,0:T(8,128)S(1)}, bf16[256,256]{1,0:T(8,128)(2,1)S(1)}, bf16[256,256]{1,0:T(8,128)(2,1)S(1)}, bf16[256,256]{1,0:T(8,128)(2,1)S...) custom-call(f32[5]{0:T(128)S(1)} %copy-done, f32[9]{0:T(128)S(1)} %copy-done.1, ...), custom_call_target="tpu_custom_call" | custom-call | tf_op jit(solution)/shard_map/pallas_call | solution.py:719
  29.8 0.0 collective-permute-done.3.odd
  29.8 0.5 collective-permute-done.2.even
  30.4 0.0 collective-permute-start.10
  30.4 0.5 collective-permute-start.11
  30.9 0.8 %collective-permute-done.10.even2 = f32[16,16,128]{2,1,0:T(8,128)S(1)} collective-permute-done((f32[16,16,128]{2,1,0:T(8,128)S(1)}, f32[16,16,128]{2,1,0:T(8,128)S(1)}, u32[]{:S(2)}, u32[]{:S(2)}) %collective-permute-start.10) | collective-permute-done | bytes 131104 | tf_op jit(solution)/shard_map/ppermute | solution.py:137
  31.7 0.2 collective-permute-done.11.odd2
  31.9 1.3 %shard_map.63 = (f32[32,48,128]{2,1,0:T(8,128)S(1)}, f32[32,40,128]{2,1,0:T(8,128)S(1)}) custom-call(f32[14,8,128]{2,1,0:T(8,128)S(1)} %get-tuple-element.45.taps_ref, bf16[256,256]{1,0:T(8,128)(2,1)S(1)} %get-tuple-element.46.quad_ref, f32[16,16,128]{2,1,0:T(8,128)S(1)} %get-tuple-element.41.own, f32[16,16,128]{2,1,0:T(8,128)S(1)} %collective-permute-done.2.even, ...), custom_call_target="tpu_custom_call" | custom-call | tf_op jit(solution)/shard_map/pallas_call | solution.py:735
  33.2 0.0 collective-permute-done.7.own2
  33.2 0.0 collective-permute-done.8.even2
  33.2 0.0 collective-permute-done.9.odd2
  33.3 1.9 %shard_map.64 = (f32[32,48,128]{2,1,0:T(8,128)S(1)}, f32[32,40,128]{2,1,0:T(8,128)S(1)}, f32[32,24,128]{2,1,0:T(8,128)S(1)}, f32[32,16,128]{2,1,0:T(8,128)S(1)}, f32[1,128]{1,0:T(1,128)S(1)}) custom-call(f32[14,8,128]{2,1,0:T(8,128)S(1)} %get-tuple-element.45.taps_ref, bf16[256,256]{1,0:T(8,128)(2,1)S(1)} %get-tuple-element.46.quad_ref, ...), custom_call_target="tpu_custom_call" | custom-call | tf_op jit(solution)/shard_map/pallas_call | solution.py:738
  35.2 1.1 %collective-permute-start.12 = (f32[32,16,128]{2,1,0:T(8,128)S(1)}, f32[32,16,128]{2,1,0:T(8,128)S(1)}, u32[]{:S(2)}, u32[]{:S(2)}) collective-permute-start(f32[32,16,128]{2,1,0:T(8,128)S(1)} %get-tuple-element.57.mine), channel_id=1, source_target_pairs={{0,5},{8,1},{16,9},{24,17},{26,25},{18,27},{10,19},{2,11},{6,3},{1... | collective-permute-start | bytes 786440 | tf_op jit(solution)/shard_map/ppermute | solution.py:157
  36.3 4.8 %collective-permute-done.12.side = f32[32,16,128]{2,1,0:T(8,128)S(1)} collective-permute-done((f32[32,16,128]{2,1,0:T(8,128)S(1)}, f32[32,16,128]{2,1,0:T(8,128)S(1)}, u32[]{:S(2)}, u32[]{:S(2)}) %collective-permute-start.12) | collective-permute-done | bytes 262176 | tf_op jit(solution)/shard_map/ppermute | solution.py:157
  41.0 0.3 collective-permute-start.13
  41.4 1.2 %shard_map.65 = (f32[32,40,128]{2,1,0:T(8,128)S(1)}, f32[32,32,128]{2,1,0:T(8,128)S(1)}, f32[32,24,128]{2,1,0:T(8,128)S(1)}) custom-call(f32[14,8,128]{2,1,0:T(8,128)S(1)} %get-tuple-element.45.taps_ref, bf16[256,256]{1,0:T(8,128)(2,1)S(1)} %get-tuple-element.46.quad_ref, f32[32,16,128]{2,1,0:T(8,128)S(1)} %get-tuple-element.57.mine, ...), custom_call_target="tpu_custom_call" | custom-call | tf_op jit(solution)/shard_map/pallas_call | solution.py:744
  42.6 0.0 collective-permute-done.13.other
  42.6 1.6 %shard_map.66 = (f32[32,40,128]{2,1,0:T(8,128)S(1)}, f32[32,32,128]{2,1,0:T(8,128)S(1)}, f32[32,24,128]{2,1,0:T(8,128)S(1)}, f32[32,16,128]{2,1,0:T(8,128)S(1)}) custom-call(f32[14,8,128]{2,1,0:T(8,128)S(1)} %get-tuple-element.45.taps_ref, ...), custom_call_target="tpu_custom_call", output_to_operand_aliasing={{0}: (6, {}), {1}: (7, {}), {2}: (8, {})} | custom-call | tf_op jit(solution)/shard_map/pallas_call | solution.py:753
  44.2 1.0 %collective-permute-start.14 = (f32[32,16,128]{2,1,0:T(8,128)S(1)}, f32[32,16,128]{2,1,0:T(8,128)S(1)}, u32[]{:S(2)}, u32[]{:S(2)}) collective-permute-start(f32[32,16,128]{2,1,0:T(8,128)S(1)} %get-tuple-element.62.mine), channel_id=1, source_target_pairs={{0,5},{8,1},{16,9},{24,17},{26,25},{18,27},{10,19},{2,11},{6,3},{1... | collective-permute-start | bytes 786440 | tf_op jit(solution)/shard_map/ppermute | solution.py:157
  45.3 0.5 shard_map.67.gaps
  45.8 4.3 %collective-permute-done.14.side = f32[32,16,128]{2,1,0:T(8,128)S(1)} collective-permute-done((f32[32,16,128]{2,1,0:T(8,128)S(1)}, f32[32,16,128]{2,1,0:T(8,128)S(1)}, u32[]{:S(2)}, u32[]{:S(2)}) %collective-permute-start.14) | collective-permute-done | bytes 262176 | tf_op jit(solution)/shard_map/ppermute | solution.py:157
  50.1 0.3 collective-permute-start.15
  50.4 1.2 %shard_map.68 = (f32[32,40,128]{2,1,0:T(8,128)S(1)}, f32[32,32,128]{2,1,0:T(8,128)S(1)}, f32[32,24,128]{2,1,0:T(8,128)S(1)}) custom-call(f32[14,8,128]{2,1,0:T(8,128)S(1)} %get-tuple-element.45.taps_ref, bf16[256,256]{1,0:T(8,128)(2,1)S(1)} %get-tuple-element.46.quad_ref, f32[32,16,128]{2,1,0:T(8,128)S(1)} %get-tuple-element.62.mine, ...), custom_call_target="tpu_custom_call" | custom-call | tf_op jit(solution)/shard_map/pallas_call | solution.py:744
  51.6 0.0 collective-permute-done.15.other
  51.6 3.0 %shard_map.69 = (f32[32,40,128]{2,1,0:T(8,128)S(1)}, f32[32,32,128]{2,1,0:T(8,128)S(1)}, f32[32,24,128]{2,1,0:T(8,128)S(1)}, f32[784,128]{1,0:T(8,128)S(1)}) custom-call(f32[14,8,128]{2,1,0:T(8,128)S(1)} %get-tuple-element.45.taps_ref, ...), custom_call_target="tpu_custom_call", output_to_operand_aliasing={{0}: (11, {}), {1}: (12, {}), {2}: (13, {})} | custom-call | tf_op jit(solution)/shard_map/pallas_call | solution.py:762
  54.7 17.1 %all_to_all.11 = f32[784,1,128]{2,1,0:T(1,128)S(1)} all-to-all(f32[784,1,128]{2,1,0:T(1,128)S(1)} %bitcast.13), channel_id=1, replica_groups=mesh['gx'=4,'gy'=4,'gz'=2] {'gx','gy'}, dimensions={0} | all-to-all | bytes 802816 | tf_op jit(solution)/shard_map/all_to_all | solution.py:162
  71.7 0.4 shard_map.70
  72.1 0.1 collective-permute-start.16
  72.2 1.6 %shard_map.71 = (f32[6]{0:T(128)}, f32[3,8,32,128]{3,2,1,0:T(8,128)}) custom-call(bf16[256,256]{1,0:T(8,128)(2,1)S(1)} %get-tuple-element.42.high_ref, bf16[256,256]{1,0:T(8,128)(2,1)S(1)} %get-tuple-element.43.low_ref, f32[784,128]{1,0:T(8,128)S(1)} %bitcast.10), custom_call_target="tpu_custom_call" | custom-call | tf_op jit(solution)/shard_map/pallas_call | solution.py:773
  73.8 0.0 collective-permute-done.16.recv_ref
  73.8 0.7 shard_map.72
Async XLA Ops:
  0.6 1.8 %collective-permute-start = (f32[8,32,128]{2,1,0:T(8,128)}, f32[8,32,128]{2,1,0:T(8,128)S(1)}, u32[]{:S(2)}, u32[]{:S(2)}) collective-permute-start(f32[8,32,128]{2,1,0:T(8,128)} %src_hbm.1), channel_id=1, source_target_pairs={{0,1},{1,0},{8,9},{9,8},{16,17},{17,16},{24,25},{25,24},{26,27},{2... | collective-permute-start | bytes 393224 | tf_op jit(solution)/shard_map/ppermute | solution.py:137
  1.2 1.6 %collective-permute-start.1 = (f32[8,32,128]{2,1,0:T(8,128)}, f32[8,32,128]{2,1,0:T(8,128)S(1)}, u32[]{:S(2)}, u32[]{:S(2)}) collective-permute-start(f32[8,32,128]{2,1,0:T(8,128)} %tgt_hbm.1), channel_id=1, source_target_pairs={{0,1},{1,0},{8,9},{9,8},{16,17},{17,16},{24,25},{25,24},{26,27},{2... | collective-permute-start | bytes 393224 | tf_op jit(solution)/shard_map/ppermute | solution.py:137
  21.5 7.6 %copy-start = (f32[5]{0:T(128)S(1)}, f32[5]{0:T(128)}, u32[]{:S(2)}) copy-start(f32[5]{0:T(128)} %k_ref.1) | copy-start | bytes 64
  21.5 7.5 %copy-start.1 = (f32[9]{0:T(128)S(1)}, f32[9]{0:T(128)}, u32[]{:S(2)}) copy-start(f32[9]{0:T(128)} %s_ref.1) | copy-start | bytes 112
  21.5 5.9 %collective-permute-start.5 = (f32[17,16,128]{2,1,0:T(8,128)S(1)}, f32[17,16,128]{2,1,0:T(8,128)S(1)}, u32[]{:S(2)}, u32[]{:S(2)}) collective-permute-start(f32[17,16,128]{2,1,0:T(8,128)S(1)} %get-tuple-element.49.own), channel_id=1, source_target_pairs={{0,4},{1,5},{8,16},{9,17},{16,8},{17,9},{24,26},{25,27},{26,24},{2... | collective-permute-start | bytes 417800 | tf_op jit(solution)/shard_map/ppermute | solution.py:151
  22.5 6.0 %collective-permute-start.4 = (f32[17,16,128]{2,1,0:T(8,128)S(1)}, f32[17,16,128]{2,1,0:T(8,128)S(1)}, u32[]{:S(2)}, u32[]{:S(2)}) collective-permute-start(f32[17,16,128]{2,1,0:T(8,128)S(1)} %get-tuple-element.49.own), channel_id=1, source_target_pairs={{0,8},{1,9},{8,0},{9,1},{16,24},{17,25},{24,16},{25,17},{26,18},{2... | collective-permute-start | bytes 417800 | tf_op jit(solution)/shard_map/ppermute | solution.py:142
  22.8 2.2 %collective-permute-start.6 = (f32[16,16,128]{2,1,0:T(8,128)S(1)}, f32[16,16,128]{2,1,0:T(8,128)S(1)}, u32[]{:S(2)}, u32[]{:S(2)}) collective-permute-start(f32[16,16,128]{2,1,0:T(8,128)S(1)} %get-tuple-element.41.own), channel_id=1, source_target_pairs={{0,1},{1,0},{8,9},{9,8},{16,17},{17,16},{24,25},{25,24},{26,27},{2... | collective-permute-start | bytes 393224 | tf_op jit(solution)/shard_map/ppermute | solution.py:137
  22.8 7.1 %collective-permute-start.3 = (f32[16,16,128]{2,1,0:T(8,128)S(1)}, f32[16,16,128]{2,1,0:T(8,128)S(1)}, u32[]{:S(2)}, u32[]{:S(2)}) collective-permute-start(f32[16,16,128]{2,1,0:T(8,128)S(1)} %get-tuple-element.41.own), channel_id=1, source_target_pairs={{0,4},{1,5},{8,16},{9,17},{16,8},{17,9},{24,26},{25,27},{26,24},{2... | collective-permute-start | bytes 393224 | tf_op jit(solution)/shard_map/ppermute | solution.py:151
  23.8 6.6 %collective-permute-start.2 = (f32[16,16,128]{2,1,0:T(8,128)S(1)}, f32[16,16,128]{2,1,0:T(8,128)S(1)}, u32[]{:S(2)}, u32[]{:S(2)}) collective-permute-start(f32[16,16,128]{2,1,0:T(8,128)S(1)} %get-tuple-element.41.own), channel_id=1, source_target_pairs={{0,8},{1,9},{8,0},{9,1},{16,24},{17,25},{24,16},{25,17},{26,18},{2... | collective-permute-start | bytes 393224 | tf_op jit(solution)/shard_map/ppermute | solution.py:142
  25.0 8.2 %collective-permute-start.7 = (f32[17,16,128]{2,1,0:T(8,128)S(1)}, f32[17,16,128]{2,1,0:T(8,128)S(1)}, u32[]{:S(2)}, u32[]{:S(2)}) collective-permute-start(f32[17,16,128]{2,1,0:T(8,128)S(1)} %get-tuple-element.49.own), channel_id=1, source_target_pairs={{0,1},{1,0},{8,9},{9,8},{16,17},{17,16},{24,25},{25,24},{26,27},{2... | collective-permute-start | bytes 417800 | tf_op jit(solution)/shard_map/ppermute | solution.py:137
  28.5 4.7 %collective-permute-start.8 = (f32[17,16,128]{2,1,0:T(8,128)S(1)}, f32[17,16,128]{2,1,0:T(8,128)S(1)}, u32[]{:S(2)}, u32[]{:S(2)}) collective-permute-start(f32[17,16,128]{2,1,0:T(8,128)S(1)} %collective-permute-done.4.even), channel_id=1, source_target_pairs={{0,1},{1,0},{8,9},{9,8},{16,17},{17,16},{24,25},{25,24},{26,27},{2... | collective-permute-start | bytes 417800 | tf_op jit(solution)/shard_map/ppermute | solution.py:137
  28.5 4.7 %collective-permute-start.9 = (f32[17,16,128]{2,1,0:T(8,128)S(1)}, f32[17,16,128]{2,1,0:T(8,128)S(1)}, u32[]{:S(2)}, u32[]{:S(2)}) collective-permute-start(f32[17,16,128]{2,1,0:T(8,128)S(1)} %collective-permute-done.5.odd), channel_id=1, source_target_pairs={{0,1},{1,0},{8,9},{9,8},{16,17},{17,16},{24,25},{25,24},{26,27},{2... | collective-permute-start | bytes 417800 | tf_op jit(solution)/shard_map/ppermute | solution.py:137
  30.4 1.3 %collective-permute-start.10 = (f32[16,16,128]{2,1,0:T(8,128)S(1)}, f32[16,16,128]{2,1,0:T(8,128)S(1)}, u32[]{:S(2)}, u32[]{:S(2)}) collective-permute-start(f32[16,16,128]{2,1,0:T(8,128)S(1)} %collective-permute-done.2.even), channel_id=1, source_target_pairs={{0,1},{1,0},{8,9},{9,8},{16,17},{17,16},{24,25},{25,24},{26,27},{2... | collective-permute-start | bytes 393224 | tf_op jit(solution)/shard_map/ppermute | solution.py:137
  30.4 1.5 %collective-permute-start.11 = (f32[16,16,128]{2,1,0:T(8,128)S(1)}, f32[16,16,128]{2,1,0:T(8,128)S(1)}, u32[]{:S(2)}, u32[]{:S(2)}) collective-permute-start(f32[16,16,128]{2,1,0:T(8,128)S(1)} %collective-permute-done.3.odd), channel_id=1, source_target_pairs={{0,1},{1,0},{8,9},{9,8},{16,17},{17,16},{24,25},{25,24},{26,27},{2... | collective-permute-start | bytes 393224 | tf_op jit(solution)/shard_map/ppermute | solution.py:137
  35.2 5.9 %collective-permute-start.12 = (f32[32,16,128]{2,1,0:T(8,128)S(1)}, f32[32,16,128]{2,1,0:T(8,128)S(1)}, u32[]{:S(2)}, u32[]{:S(2)}) collective-permute-start(f32[32,16,128]{2,1,0:T(8,128)S(1)} %get-tuple-element.57.mine), channel_id=1, source_target_pairs={{0,5},{8,1},{16,9},{24,17},{26,25},{18,27},{10,19},{2,11},{6,3},{1... | collective-permute-start | bytes 786440 | tf_op jit(solution)/shard_map/ppermute | solution.py:157
  41.0 1.6 %collective-permute-start.13 = (f32[32,16,128]{2,1,0:T(8,128)S(1)}, f32[32,16,128]{2,1,0:T(8,128)S(1)}, u32[]{:S(2)}, u32[]{:S(2)}) collective-permute-start(f32[32,16,128]{2,1,0:T(8,128)S(1)} %collective-permute-done.12.side), channel_id=1, source_target_pairs={{0,1},{1,0},{8,9},{9,8},{16,17},{17,16},{24,25},{25,24},{26,27},{2... | collective-permute-start | bytes 786440 | tf_op jit(solution)/shard_map/ppermute | solution.py:137
  44.2 5.9 %collective-permute-start.14 = (f32[32,16,128]{2,1,0:T(8,128)S(1)}, f32[32,16,128]{2,1,0:T(8,128)S(1)}, u32[]{:S(2)}, u32[]{:S(2)}) collective-permute-start(f32[32,16,128]{2,1,0:T(8,128)S(1)} %get-tuple-element.62.mine), channel_id=1, source_target_pairs={{0,5},{8,1},{16,9},{24,17},{26,25},{18,27},{10,19},{2,11},{6,3},{1... | collective-permute-start | bytes 786440 | tf_op jit(solution)/shard_map/ppermute | solution.py:157
  50.1 1.5 %collective-permute-start.15 = (f32[32,16,128]{2,1,0:T(8,128)S(1)}, f32[32,16,128]{2,1,0:T(8,128)S(1)}, u32[]{:S(2)}, u32[]{:S(2)}) collective-permute-start(f32[32,16,128]{2,1,0:T(8,128)S(1)} %collective-permute-done.14.side), channel_id=1, source_target_pairs={{0,1},{1,0},{8,9},{9,8},{16,17},{17,16},{24,25},{25,24},{26,27},{2... | collective-permute-start | bytes 786440 | tf_op jit(solution)/shard_map/ppermute | solution.py:137
  72.1 1.7 %collective-permute-start.16 = (f32[3,4,32,128]{3,2,1,0:T(8,128)S(1)}, f32[3,4,32,128]{3,2,1,0:T(8,128)S(1)}, u32[]{:S(2)}, u32[]{:S(2)}) collective-permute-start(f32[3,4,32,128]{3,2,1,0:T(8,128)S(1)} %bitcast.14), channel_id=1, source_target_pairs={{0,1},{1,0},{8,9},{9,8},{16,17},{17,16},{24,25},{25,24},{26,27},{2... | collective-permute-start | bytes 589832 | tf_op jit(solution)/shard_map/ppermute | solution.py:137
where the time goes:
time: 74.7 us; the launch traced here: 74.5 us
  blocking collectives  35.4 us (47%)
  Pallas kernels  15.8 us (21%)
  waiting for transfers between devices  14.5 us (19%)
  starting transfers between devices  7.94 us (11%)
  between operations  0.82 us (1%)
    all_to_all x2, blocking collectives, trade_chunks(): lax.all_to_all(value.reshape(rows, 1, lanes), ('gx', 'gy'), 0, 0, tiled=T...  35.4 us
    ppermute x2, waiting for transfers between devices, swap_sides(): return lax.ppermute(value, AXES, pairs)  9.1 us
    pallas_call x1, Pallas kernels, slab_shards(): call(bind(last_kernel), [v_shape, u_shape, v2_shape, f32(Pn * (3 * S + 1)...  3.01 us
    pallas_call x2, Pallas kernels, early(): call(bind(early_kernel), [v_shape, u_shape, v2_shape], 0, 6, [vm(X, S + H...  2.46 us
    ppermute x2, waiting for transfers between devices, swap_odd(): return lax.ppermute(value, AXES, pairs)  2.39 us
    ppermute x11, starting transfers between devices, swap_cores(): return lax.ppermute(value, AXES, pairs)  2.32 us
    ppermute x2, starting transfers between devices, swap_sides(): return lax.ppermute(value, AXES, pairs)  2.13 us
    ppermute x2, starting transfers between devices, swap_odd(): return lax.ppermute(value, AXES, pairs)  1.99 us
  transfers between devices with their start and end apart: 17, of which 8 were waited for; matrix products, arithmetic and copies ran while one was open for 0% of the time, Pallas kernels for 10%

commit v1 on v0

--- a/solution.py
+++ b/solution.py
@@ -114,7 +114,7 @@
             and self.bx == 2 * self.gs
             and self.Z == self.P * self.S
             and self.S == self.H
-            and self.S % 8 == 0
+            and self.S % 16 == 0
             and self.R % 4 == 0
             and ITERS == 6
         )
@@ -157,9 +157,9 @@
     return lax.ppermute(value, AXES, pairs)
 
 
-def trade_chunks(value):
+def trade_chunks(value, axes):
     rows, lanes = value.shape
-    out = lax.all_to_all(value.reshape(rows, 1, lanes), ("gx", "gy"), 0, 0, tiled=True)
+    out = lax.all_to_all(value.reshape(rows, 1, lanes), axes, 0, 0, tiled=True)
     return out.reshape(rows, lanes)
 
 
@@ -256,12 +256,12 @@
             for xx, value in enumerate(turn_groups(plan, parts)):
                 out_ref[i * gs + xx] = value
     t_ref[XH] = jnp.zeros((S, LANES), jnp.float32)
-    t_ref[XH, :1, :] = sum_rows(plan, in_ref, size)
-
-
-def sum_rows(plan, ref, size):
+    t_ref[XH, :1, :] = sum_rows(in_ref, size)
+
+
+def sum_rows(ref, size):
     total = ref[size - 1 : size, :]
-    for p in range(1, plan.P):
+    for p in range(1, ref.shape[0] // size):
         total = total + ref[size * p + size - 1 : size * p + size, :]
     return total
 
@@ -320,7 +320,7 @@
     return total
 
 
-MANY = 8
+MANY = 16
 
 
 def run_passes(plan, passes):
@@ -409,6 +409,8 @@
 
 def gaps_of(plan, tot, tw, olds, news):
     S = plan.S
+    half = S // 2
+    mine = pl.multiple_of(half * lax.axis_index("gz"), 8)
     first_half = lane_at() < LANES // 2
     both = tot[:1, :]
     sum_s = jnp.sum(jnp.where(first_half, both, 0.0), axis=1, keepdims=True)
@@ -416,21 +418,26 @@
     scale_s = plan.cells / jnp.broadcast_to(sum_s, (1, LANES))
     scale_t = plan.cells / jnp.broadcast_to(sum_t, (1, LANES))
 
-    def mid(ref, x):
+    def mid(ref):
         edge = (ref.shape[1] - S) // 2
-        return ref[x, edge : edge + S, :]
+        ref = ref.at[:, pl.ds(mine, ref.shape[1] - half), :]
+        return lambda x: ref[x, edge : edge + half, :]
+
+    t_at = mid(tw)
+    olds = [old if old is None else mid(old) for old in olds]
+    news = [mid(new) for new in news]
 
     def p_step(x, carry):
-        t = mid(tw, x)
+        t = t_at(x)
         want = scale_t * t
         have = scale_s * t
         result = []
         for part, old, new in zip(carry, olds, news):
-            value = have / mid(new, x)
+            value = have / new(x)
             if old is not None:
-                value = value * mid(old, x)
+                value = value * old(x)
             gap = jnp.abs(value - want)
-            for r in range(0, S, 8):
+            for r in range(0, half, 8):
                 part = part + gap[r : r + 8]
             result.append(part)
         return tuple(result)
@@ -592,8 +599,9 @@
 def last_kernel(plan, taps_ref, quad_ref, slope_ref, smooth_ref, mine, other, sw, tw, prev,
                 gaps, tot, v_in, u_in, v2_in, v, u, v2, out_ref, win, zb, zc, zg, raw):
     del v_in, u_in, v2_in
-    R, S, X, gs, Q = plan.R, plan.S, plan.X, plan.gs, plan.Q
-    size = 3 * S + 1
+    R, S, H, X, gs, Q = plan.R, plan.S, plan.H, plan.X, plan.gs, plan.Q
+    half = S // 2
+    size = 3 * half + 1
     c = lax.axis_index("gz")
     at = place_of(plan)
     taps = kernel_taps(plan, taps_ref)
@@ -603,21 +611,42 @@
     clear_edges(zg, R, X)
     for comp in range(3):
         clear_edges(raw.at[comp], Q, X)
-    passes = late_rows(plan, at, taps, quad_ref, mine, other, sw, tw, v, u, v2, win, zb, zc)
+    real = jnp.where(jnp.where(c == 1, at > 0, at < plan.P - 1), 1.0, 0.0)
+
+    @pl.when(c == 0)
+    def _():
+        win[:, :half, :] = mine[:, half:, :]
+        win[:, half:, :] = other[:, :half, :] * real
+
+    @pl.when(c == 1)
+    def _():
+        win[:, :half, :] = other[:, H - half :, :] * real
+        win[:, half:, :] = mine[:, :half, :]
+
+    step = functools.partial(scale_step, plan, at, taps, quad_ref)
+    own = pl.multiple_of(half * c, 8)
+    first = pl.multiple_of(S + half - S * c, 8)
+    second = pl.multiple_of(S - half * c, 8)
+    passes = [
+        step(zb, win, 0, v, tw, R, first, half),
+        step(zc, v, second, u, sw, 2 * R, second, half),
+        step(zb, u, half, v2, tw, 3 * R, half, half),
+    ]
+    near = v2.at[:, pl.ds(own, S), :]
 
     def z_part(base):
         for x in range(base, base + MANY):
-            load = lambda j: v2[x, j : j + S, :]
-            zc[R + x, :S, :] = unit_sum(load, taps, R)
-            zg[R + x, :S, :] = odd_sum(load, taps, R)
+            load = lambda j: near[x, j : j + half, :]
+            zc[R + x, :half, :] = unit_sum(load, taps, R)
+            zg[R + x] = odd_sum(load, taps, R)
 
     def matmul_part(base):
         kk, gk, kg = [], [], []
         for q in range(MANY):
-            flat = lambda j: zc[base + q + j, :S, :]
+            flat = lambda j: zc[base + q + j, :half, :]
             kk.append(unit_sum(flat, taps, R))
             gk.append(odd_sum(flat, taps, R))
-            kg.append(unit_sum(lambda j: zg[base + q + j, :S, :], taps, R))
+            kg.append(unit_sum(lambda j: zg[base + q + j], taps, R))
         kk, gk, kg = (jnp.concatenate(part, axis=0) for part in (kk, gk, kg))
         nums = lanes_times(gk, quad_ref), lanes_times(kk, slope_ref), lanes_times(kg, quad_ref)
         return lanes_times(kk, quad_ref), nums
@@ -627,36 +656,36 @@
         for comp, num in enumerate(nums):
             value = num / kvol
             for q in range(MANY):
-                raw[comp, Q + base + q] = value[q * S : (q + 1) * S]
+                raw[comp, Q + base + q] = value[q * half : (q + 1) * half]
 
     run_passes(plan, passes + [(z_part, matmul_part, emit_part)])
 
     for i in range(plan.nx):
-        x = plan.bx * i + gs * c
         for comp in range(3):
-            parts = []
-            for xx in range(gs):
-                parts.append(even_sum(lambda j: raw[comp, x + xx + j], stap, Q))
+            x = plan.bx * i
+            parts = [even_sum(lambda j: raw[comp, x + k + j], stap, Q) for k in range(plan.bx)]
             flat = lanes_times(jnp.concatenate(parts, axis=0), smooth_ref)
-            turned = turn_groups(plan, [flat[xx * S : (xx + 1) * S] for xx in range(gs)])
-            for j in range(plan.ny):
-                base = size * (i * plan.ny + j) + comp * S
-                out_ref[base : base + S, :] = turned[j]
+            for core in range(2):
+                rows = range(gs * core, gs * (core + 1))
+                turned = turn_groups(plan, [flat[k * half : (k + 1) * half] for k in rows])
+                for j in range(plan.ny):
+                    base = size * ((i * plan.ny + j) * 2 + core) + comp * half
+                    out_ref[base : base + half, :] = turned[j]
 
     rows = gaps_of(plan, tot, tw, (prev, v), (v, v2))
     stat = gaps[...] + in_lanes(rows, ITERS - 2)
-    for p in range(plan.P):
-        out_ref[size * p + 3 * S : size * (p + 1), :] = stat
+    for p in range(2 * plan.P):
+        out_ref[size * (p + 1) - 1 : size * (p + 1), :] = stat
 
 
 def smooth_z(plan, core, high_ref, low_ref, in_ref, data, emit):
-    S = plan.S
-    size = 3 * S + 1
-    for place in range(plan.P):
+    half = plan.S // 2
+    size = 3 * half + 1
+    for part in range(2 * plan.P):
         for comp in range(3):
-            base = size * plan.chip(place) + comp * S
-            data[S * place : S * place + S, comp * LANES : (comp + 1) * LANES] = in_ref[
-                base : base + S, :
+            base = size * plan.device(part // 2, part % 2) + comp * half
+            data[half * part : half * (part + 1), comp * LANES : (comp + 1) * LANES] = in_ref[
+                base : base + half, :
             ]
     rows = pl.ds(pl.multiple_of(core * LANES, LANES), LANES)
     m_high, m_low = high_ref[rows, :], low_ref[rows, :]
@@ -684,7 +713,7 @@
     smooth_z(plan, c, high_ref, low_ref, in_ref, data, emit)
     copy = pltpu.make_async_copy(keep, out_hbm.at[:, pl.ds(gs * c, gs)], sem)
     copy.start()
-    gone = sum_rows(plan, in_ref, 3 * plan.S + 1) / plan.cells
+    gone = sum_rows(in_ref, 3 * plan.S // 2 + 1) / plan.cells
     for t in range(ITERS):
         mis_ref[t] = jnp.sum(jnp.where(lane_at() == t, gone, 0.0))
     copy.wait()
@@ -710,7 +739,7 @@
     (chunks,) = call(
         bind(chunk_kernel), [f32(Pn * (2 * S + 1), LANES)], 0, 4, [vm(*half.shape)]
     )(keep, swap_cores(plan, source), swap_cores(plan, target), stat)
-    spread = trade_chunks(chunks)
+    spread = trade_chunks(chunks, ("gx", "gy"))
     own_s, own_t = call(
         bind(unpack_kernel), [f32(XH, S, LANES), f32(XH + 1, S, LANES)], 0, 1
     )(spread)
@@ -760,11 +789,11 @@
     other = swap_cores(plan, side)
     v5, u6, v6 = early(u, side)
     *_, chunks = call(
-        bind(last_kernel), [v_shape, u_shape, v2_shape, f32(Pn * (3 * S + 1), LANES)], 0, 14,
-        [rest, zb, zb, vm(X + 2 * R, S, LANES), vm(3, X + 2 * plan.Q, S, LANES)],
+        bind(last_kernel), [v_shape, u_shape, v2_shape, f32(2 * Pn * (3 * S // 2 + 1), LANES)], 0, 14,
+        [vm(X, S, LANES), zb, zb, vm(X + 2 * R, S // 2, LANES), vm(3, X + 2 * plan.Q, S // 2, LANES)],
         aliases={11: 0, 12: 1, 13: 2},
     )(taps, quad_k, quad_g, quad_s, u, other, sw, tw, v4, gaps, tot, v5, u6, v6)
-    spread = trade_chunks(chunks)
+    spread = trade_chunks(chunks, AXES)
     data = vm(Z, 3 * LANES)
     (send,) = call(bind(away_kernel), [f32(3, LANES, LANES)], 0, 3, [data])(high, low, spread)
     half = (3, plan.gs, plan.by, LANES)

time: 74.7 us -> 73 us (0.977)
  Pallas kernels: 15.8 us -> 14.5 us
    pallas_call x1, Pallas kernels: 3.01 us -> 2.09 us  [slab_shards(): call(bind(last_kernel), [v_shape, u_shape, v2_shape, f32(2 * Pn * (3 * S...]
where the time goes in v1:
time: 73 us; the launch traced here: 72.8 us
  blocking collectives  34.8 us (48%)
  waiting for transfers between devices  14.6 us (20%)
  Pallas kernels  14.5 us (20%)
  starting transfers between devices  8.07 us (11%)
  between operations  0.81 us (1%)
    all_to_all x2, blocking collectives, trade_chunks(): out = lax.all_to_all(value.reshape(rows, 1, lanes), axes, 0, 0, tiled=True)  34.8 us
    ppermute x2, waiting for transfers between devices, swap_sides(): return lax.ppermute(value, AXES, pairs)  9.13 us
    ppermute x2, waiting for transfers between devices, swap_odd(): return lax.ppermute(value, AXES, pairs)  2.39 us
    ppermute x11, starting transfers between devices, swap_cores(): return lax.ppermute(value, AXES, pairs)  2.38 us
    pallas_call x2, Pallas kernels, early(): call(bind(early_kernel), [v_shape, u_shape, v2_shape], 0, 6, [vm(X, S + H...  2.32 us
    ppermute x2, starting transfers between devices, swap_sides(): return lax.ppermute(value, AXES, pairs)  2.19 us
    pallas_call x1, Pallas kernels, slab_shards(): call(bind(last_kernel), [v_shape, u_shape, v2_shape, f32(2 * Pn * (3 * S...  2.09 us
    ppermute x2, starting transfers between devices, swap_odd(): return lax.ppermute(value, AXES, pairs)  1.99 us
  transfers between devices with their start and end apart: 17, of which 8 were waited for; matrix products, arithmetic and copies ran while one was open for 0% of the time, Pallas kernels for 10%

profile of v1, /device:TPU:0, one launch (start us, length us, event | category | flops | bytes accessed | tf_op | source)
XLA Modules:
  0.0 72.8 jit_solution(9783352875186814387)
XLA Ops:
  0.6 0.6 collective-permute-start
  1.2 0.1 collective-permute-start.1
  1.3 1.2 %shard_map.59 = (f32[2,128,128]{2,1,0:T(8,128)S(1)}, f32[1,128]{1,0:T(1,128)S(1)}) custom-call(f32[8,32,128]{2,1,0:T(8,128)} %src_hbm.1, f32[8,32,128]{2,1,0:T(8,128)} %tgt_hbm.1), custom_call_target="tpu_custom_call" | custom-call | tf_op jit(solution)/shard_map/pallas_call | solution.py:735
  2.5 0.0 collective-permute-done.src_ref
  2.5 0.3 collective-permute-done.1.tgt_ref
  2.7 0.1 shard_map.60
  2.9 18.4 %all_to_all.10 = f32[528,1,128]{2,1,0:T(1,128)S(1)} all-to-all(f32[528,1,128]{2,1,0:T(1,128)S(1)} %bitcast.11), channel_id=1, replica_groups=mesh['gx'=4,'gy'=4,'gz'=2] {'gx','gy'}, dimensions={0} | all-to-all | bytes 540672 | tf_op jit(solution)/shard_map/all_to_all | solution.py:162
  21.2 0.3 shard_map.61
  21.5 0.0 copy-start
  21.5 0.0 copy-start.1
  21.5 1.0 %collective-permute-start.5 = (f32[17,16,128]{2,1,0:T(8,128)S(1)}, f32[17,16,128]{2,1,0:T(8,128)S(1)}, u32[]{:S(2)}, u32[]{:S(2)}) collective-permute-start(f32[17,16,128]{2,1,0:T(8,128)S(1)} %get-tuple-element.49.own), channel_id=1, source_target_pairs={{0,4},{1,5},{8,16},{9,17},{16,8},{17,9},{24,26},{25,27},{26,24},{2... | collective-permute-start | bytes 417800 | tf_op jit(solution)/shard_map/ppermute | solution.py:151
  22.5 0.3 collective-permute-start.4
  22.8 0.0 collective-permute-start.6
  22.8 1.0 %collective-permute-start.3 = (f32[16,16,128]{2,1,0:T(8,128)S(1)}, f32[16,16,128]{2,1,0:T(8,128)S(1)}, u32[]{:S(2)}, u32[]{:S(2)}) collective-permute-start(f32[16,16,128]{2,1,0:T(8,128)S(1)} %get-tuple-element.41.own), channel_id=1, source_target_pairs={{0,4},{1,5},{8,16},{9,17},{16,8},{17,9},{24,26},{25,27},{26,24},{2... | collective-permute-start | bytes 393224 | tf_op jit(solution)/shard_map/ppermute | solution.py:151
  23.8 1.2 %collective-permute-start.2 = (f32[16,16,128]{2,1,0:T(8,128)S(1)}, f32[16,16,128]{2,1,0:T(8,128)S(1)}, u32[]{:S(2)}, u32[]{:S(2)}) collective-permute-start(f32[16,16,128]{2,1,0:T(8,128)S(1)} %get-tuple-element.41.own), channel_id=1, source_target_pairs={{0,8},{1,9},{8,0},{9,1},{16,24},{17,25},{24,16},{25,17},{26,18},{2... | collective-permute-start | bytes 393224 | tf_op jit(solution)/shard_map/ppermute | solution.py:142
  25.0 0.0 collective-permute-done.6.own2
  25.0 0.0 collective-permute-start.7
  25.0 2.4 %collective-permute-done.5.odd = f32[17,16,128]{2,1,0:T(8,128)S(1)} collective-permute-done((f32[17,16,128]{2,1,0:T(8,128)S(1)}, f32[17,16,128]{2,1,0:T(8,128)S(1)}, u32[]{:S(2)}, u32[]{:S(2)}) %collective-permute-start.5) | collective-permute-done | bytes 139296 | tf_op jit(solution)/shard_map/ppermute | solution.py:151
  27.4 1.1 %collective-permute-done.4.even = f32[17,16,128]{2,1,0:T(8,128)S(1)} collective-permute-done((f32[17,16,128]{2,1,0:T(8,128)S(1)}, f32[17,16,128]{2,1,0:T(8,128)S(1)}, u32[]{:S(2)}, u32[]{:S(2)}) %collective-permute-start.4) | collective-permute-done | bytes 139296 | tf_op jit(solution)/shard_map/ppermute | solution.py:142
  28.5 0.0 collective-permute-start.8
  28.5 0.5 collective-permute-start.9
  29.0 0.0 copy-done
  29.0 0.0 copy-done.1
  29.0 0.8 %shard_map.62 = (f32[14,8,128]{2,1,0:T(8,128)S(1)}, bf16[256,256]{1,0:T(8,128)(2,1)S(1)}, bf16[256,256]{1,0:T(8,128)(2,1)S(1)}, bf16[256,256]{1,0:T(8,128)(2,1)S...) custom-call(f32[5]{0:T(128)S(1)} %copy-done, f32[9]{0:T(128)S(1)} %copy-done.1, ...), custom_call_target="tpu_custom_call" | custom-call | tf_op jit(solution)/shard_map/pallas_call | solution.py:748
  29.8 0.0 collective-permute-done.3.odd
  29.8 0.5 collective-permute-done.2.even
  30.4 0.0 collective-permute-start.10
  30.4 0.5 collective-permute-start.11
  30.9 0.8 %collective-permute-done.10.even2 = f32[16,16,128]{2,1,0:T(8,128)S(1)} collective-permute-done((f32[16,16,128]{2,1,0:T(8,128)S(1)}, f32[16,16,128]{2,1,0:T(8,128)S(1)}, u32[]{:S(2)}, u32[]{:S(2)}) %collective-permute-start.10) | collective-permute-done | bytes 131104 | tf_op jit(solution)/shard_map/ppermute | solution.py:137
  31.7 0.2 collective-permute-done.11.odd2
  31.9 1.3 %shard_map.63 = (f32[32,48,128]{2,1,0:T(8,128)S(1)}, f32[32,40,128]{2,1,0:T(8,128)S(1)}) custom-call(f32[14,8,128]{2,1,0:T(8,128)S(1)} %get-tuple-element.45.taps_ref, bf16[256,256]{1,0:T(8,128)(2,1)S(1)} %get-tuple-element.46.quad_ref, f32[16,16,128]{2,1,0:T(8,128)S(1)} %get-tuple-element.41.own, f32[16,16,128]{2,1,0:T(8,128)S(1)} %collective-permute-done.2.even, ...), custom_call_target="tpu_custom_call" | custom-call | tf_op jit(solution)/shard_map/pallas_call | solution.py:764
  33.2 0.0 collective-permute-done.7.own2
  33.2 0.0 collective-permute-done.8.even2
  33.2 0.0 collective-permute-done.9.odd2
  33.2 1.9 %shard_map.64 = (f32[32,48,128]{2,1,0:T(8,128)S(1)}, f32[32,40,128]{2,1,0:T(8,128)S(1)}, f32[32,24,128]{2,1,0:T(8,128)S(1)}, f32[32,16,128]{2,1,0:T(8,128)S(1)}, f32[1,128]{1,0:T(1,128)S(1)}) custom-call(f32[14,8,128]{2,1,0:T(8,128)S(1)} %get-tuple-element.45.taps_ref, bf16[256,256]{1,0:T(8,128)(2,1)S(1)} %get-tuple-element.46.quad_ref, ...), custom_call_target="tpu_custom_call" | custom-call | tf_op jit(solution)/shard_map/pallas_call | solution.py:767
  35.1 1.1 %collective-permute-start.12 = (f32[32,16,128]{2,1,0:T(8,128)S(1)}, f32[32,16,128]{2,1,0:T(8,128)S(1)}, u32[]{:S(2)}, u32[]{:S(2)}) collective-permute-start(f32[32,16,128]{2,1,0:T(8,128)S(1)} %get-tuple-element.57.mine), channel_id=1, source_target_pairs={{0,5},{8,1},{16,9},{24,17},{26,25},{18,27},{10,19},{2,11},{6,3},{1... | collective-permute-start | bytes 786440 | tf_op jit(solution)/shard_map/ppermute | solution.py:157
  36.2 4.8 %collective-permute-done.12.side = f32[32,16,128]{2,1,0:T(8,128)S(1)} collective-permute-done((f32[32,16,128]{2,1,0:T(8,128)S(1)}, f32[32,16,128]{2,1,0:T(8,128)S(1)}, u32[]{:S(2)}, u32[]{:S(2)}) %collective-permute-start.12) | collective-permute-done | bytes 262176 | tf_op jit(solution)/shard_map/ppermute | solution.py:157
  41.0 0.3 collective-permute-start.13
  41.3 1.2 %shard_map.65 = (f32[32,40,128]{2,1,0:T(8,128)S(1)}, f32[32,32,128]{2,1,0:T(8,128)S(1)}, f32[32,24,128]{2,1,0:T(8,128)S(1)}) custom-call(f32[14,8,128]{2,1,0:T(8,128)S(1)} %get-tuple-element.45.taps_ref, bf16[256,256]{1,0:T(8,128)(2,1)S(1)} %get-tuple-element.46.quad_ref, f32[32,16,128]{2,1,0:T(8,128)S(1)} %get-tuple-element.57.mine, ...), custom_call_target="tpu_custom_call" | custom-call | tf_op jit(solution)/shard_map/pallas_call | solution.py:773
  42.5 0.0 collective-permute-done.13.other
  42.5 1.6 %shard_map.66 = (f32[32,40,128]{2,1,0:T(8,128)S(1)}, f32[32,32,128]{2,1,0:T(8,128)S(1)}, f32[32,24,128]{2,1,0:T(8,128)S(1)}, f32[32,16,128]{2,1,0:T(8,128)S(1)}) custom-call(f32[14,8,128]{2,1,0:T(8,128)S(1)} %get-tuple-element.45.taps_ref, ...), custom_call_target="tpu_custom_call", output_to_operand_aliasing={{0}: (6, {}), {1}: (7, {}), {2}: (8, {})} | custom-call | tf_op jit(solution)/shard_map/pallas_call | solution.py:782
  44.1 1.1 %collective-permute-start.14 = (f32[32,16,128]{2,1,0:T(8,128)S(1)}, f32[32,16,128]{2,1,0:T(8,128)S(1)}, u32[]{:S(2)}, u32[]{:S(2)}) collective-permute-start(f32[32,16,128]{2,1,0:T(8,128)S(1)} %get-tuple-element.62.mine), channel_id=1, source_target_pairs={{0,5},{8,1},{16,9},{24,17},{26,25},{18,27},{10,19},{2,11},{6,3},{1... | collective-permute-start | bytes 786440 | tf_op jit(solution)/shard_map/ppermute | solution.py:157
  45.2 0.4 shard_map.67.gaps
  45.6 4.4 %collective-permute-done.14.side = f32[32,16,128]{2,1,0:T(8,128)S(1)} collective-permute-done((f32[32,16,128]{2,1,0:T(8,128)S(1)}, f32[32,16,128]{2,1,0:T(8,128)S(1)}, u32[]{:S(2)}, u32[]{:S(2)}) %collective-permute-start.14) | collective-permute-done | bytes 262176 | tf_op jit(solution)/shard_map/ppermute | solution.py:157
  50.0 0.3 collective-permute-start.15
  50.3 1.2 %shard_map.68 = (f32[32,40,128]{2,1,0:T(8,128)S(1)}, f32[32,32,128]{2,1,0:T(8,128)S(1)}, f32[32,24,128]{2,1,0:T(8,128)S(1)}) custom-call(f32[14,8,128]{2,1,0:T(8,128)S(1)} %get-tuple-element.45.taps_ref, bf16[256,256]{1,0:T(8,128)(2,1)S(1)} %get-tuple-element.46.quad_ref, f32[32,16,128]{2,1,0:T(8,128)S(1)} %get-tuple-element.62.mine, ...), custom_call_target="tpu_custom_call" | custom-call | tf_op jit(solution)/shard_map/pallas_call | solution.py:773
  51.4 0.0 collective-permute-done.15.other
  51.5 2.1 %shard_map.69 = (f32[32,40,128]{2,1,0:T(8,128)S(1)}, f32[32,32,128]{2,1,0:T(8,128)S(1)}, f32[32,24,128]{2,1,0:T(8,128)S(1)}, f32[800,128]{1,0:T(8,128)S(1)}) custom-call(f32[14,8,128]{2,1,0:T(8,128)S(1)} %get-tuple-element.45.taps_ref, ...), custom_call_target="tpu_custom_call", output_to_operand_aliasing={{0}: (11, {}), {1}: (12, {}), {2}: (13, {})} | custom-call | tf_op jit(solution)/shard_map/pallas_call | solution.py:791
  53.6 16.4 %all_to_all.11 = f32[800,1,128]{2,1,0:T(1,128)S(1)} all-to-all(f32[800,1,128]{2,1,0:T(1,128)S(1)} %bitcast.13), channel_id=1, replica_groups=mesh['gx'=4,'gy'=4,'gz'=2] {'gx','gy','gz'}, dimensions={0} | all-to-all | bytes 819200 | tf_op jit(solution)/shard_map/all_to_all | solution.py:162
  70.0 0.4 shard_map.70
  70.4 0.1 collective-permute-start.16
  70.5 1.6 %shard_map.71 = (f32[6]{0:T(128)}, f32[3,8,32,128]{3,2,1,0:T(8,128)}) custom-call(bf16[256,256]{1,0:T(8,128)(2,1)S(1)} %get-tuple-element.42.high_ref, bf16[256,256]{1,0:T(8,128)(2,1)S(1)} %get-tuple-element.43.low_ref, f32[800,128]{1,0:T(8,128)S(1)} %bitcast.10), custom_call_target="tpu_custom_call" | custom-call | tf_op jit(solution)/shard_map/pallas_call | solution.py:802
  72.1 0.0 collective-permute-done.16.recv_ref
  72.1 0.7 shard_map.72
Async XLA Ops:
  0.6 1.8 %collective-permute-start = (f32[8,32,128]{2,1,0:T(8,128)}, f32[8,32,128]{2,1,0:T(8,128)S(1)}, u32[]{:S(2)}, u32[]{:S(2)}) collective-permute-start(f32[8,32,128]{2,1,0:T(8,128)} %src_hbm.1), channel_id=1, source_target_pairs={{0,1},{1,0},{8,9},{9,8},{16,17},{17,16},{24,25},{25,24},{26,27},{2... | collective-permute-start | bytes 393224 | tf_op jit(solution)/shard_map/ppermute | solution.py:137
  1.2 1.6 %collective-permute-start.1 = (f32[8,32,128]{2,1,0:T(8,128)}, f32[8,32,128]{2,1,0:T(8,128)S(1)}, u32[]{:S(2)}, u32[]{:S(2)}) collective-permute-start(f32[8,32,128]{2,1,0:T(8,128)} %tgt_hbm.1), channel_id=1, source_target_pairs={{0,1},{1,0},{8,9},{9,8},{16,17},{17,16},{24,25},{25,24},{26,27},{2... | collective-permute-start | bytes 393224 | tf_op jit(solution)/shard_map/ppermute | solution.py:137
  21.5 7.6 %copy-start = (f32[5]{0:T(128)S(1)}, f32[5]{0:T(128)}, u32[]{:S(2)}) copy-start(f32[5]{0:T(128)} %k_ref.1) | copy-start | bytes 64
  21.5 7.5 %copy-start.1 = (f32[9]{0:T(128)S(1)}, f32[9]{0:T(128)}, u32[]{:S(2)}) copy-start(f32[9]{0:T(128)} %s_ref.1) | copy-start | bytes 112
  21.5 5.9 %collective-permute-start.5 = (f32[17,16,128]{2,1,0:T(8,128)S(1)}, f32[17,16,128]{2,1,0:T(8,128)S(1)}, u32[]{:S(2)}, u32[]{:S(2)}) collective-permute-start(f32[17,16,128]{2,1,0:T(8,128)S(1)} %get-tuple-element.49.own), channel_id=1, source_target_pairs={{0,4},{1,5},{8,16},{9,17},{16,8},{17,9},{24,26},{25,27},{26,24},{2... | collective-permute-start | bytes 417800 | tf_op jit(solution)/shard_map/ppermute | solution.py:151
  22.5 6.0 %collective-permute-start.4 = (f32[17,16,128]{2,1,0:T(8,128)S(1)}, f32[17,16,128]{2,1,0:T(8,128)S(1)}, u32[]{:S(2)}, u32[]{:S(2)}) collective-permute-start(f32[17,16,128]{2,1,0:T(8,128)S(1)} %get-tuple-element.49.own), channel_id=1, source_target_pairs={{0,8},{1,9},{8,0},{9,1},{16,24},{17,25},{24,16},{25,17},{26,18},{2... | collective-permute-start | bytes 417800 | tf_op jit(solution)/shard_map/ppermute | solution.py:142
  22.8 2.2 %collective-permute-start.6 = (f32[16,16,128]{2,1,0:T(8,128)S(1)}, f32[16,16,128]{2,1,0:T(8,128)S(1)}, u32[]{:S(2)}, u32[]{:S(2)}) collective-permute-start(f32[16,16,128]{2,1,0:T(8,128)S(1)} %get-tuple-element.41.own), channel_id=1, source_target_pairs={{0,1},{1,0},{8,9},{9,8},{16,17},{17,16},{24,25},{25,24},{26,27},{2... | collective-permute-start | bytes 393224 | tf_op jit(solution)/shard_map/ppermute | solution.py:137
  22.8 7.1 %collective-permute-start.3 = (f32[16,16,128]{2,1,0:T(8,128)S(1)}, f32[16,16,128]{2,1,0:T(8,128)S(1)}, u32[]{:S(2)}, u32[]{:S(2)}) collective-permute-start(f32[16,16,128]{2,1,0:T(8,128)S(1)} %get-tuple-element.41.own), channel_id=1, source_target_pairs={{0,4},{1,5},{8,16},{9,17},{16,8},{17,9},{24,26},{25,27},{26,24},{2... | collective-permute-start | bytes 393224 | tf_op jit(solution)/shard_map/ppermute | solution.py:151
  23.8 6.6 %collective-permute-start.2 = (f32[16,16,128]{2,1,0:T(8,128)S(1)}, f32[16,16,128]{2,1,0:T(8,128)S(1)}, u32[]{:S(2)}, u32[]{:S(2)}) collective-permute-start(f32[16,16,128]{2,1,0:T(8,128)S(1)} %get-tuple-element.41.own), channel_id=1, source_target_pairs={{0,8},{1,9},{8,0},{9,1},{16,24},{17,25},{24,16},{25,17},{26,18},{2... | collective-permute-start | bytes 393224 | tf_op jit(solution)/shard_map/ppermute | solution.py:142
  25.0 8.2 %collective-permute-start.7 = (f32[17,16,128]{2,1,0:T(8,128)S(1)}, f32[17,16,128]{2,1,0:T(8,128)S(1)}, u32[]{:S(2)}, u32[]{:S(2)}) collective-permute-start(f32[17,16,128]{2,1,0:T(8,128)S(1)} %get-tuple-element.49.own), channel_id=1, source_target_pairs={{0,1},{1,0},{8,9},{9,8},{16,17},{17,16},{24,25},{25,24},{26,27},{2... | collective-permute-start | bytes 417800 | tf_op jit(solution)/shard_map/ppermute | solution.py:137
  28.5 4.7 %collective-permute-start.8 = (f32[17,16,128]{2,1,0:T(8,128)S(1)}, f32[17,16,128]{2,1,0:T(8,128)S(1)}, u32[]{:S(2)}, u32[]{:S(2)}) collective-permute-start(f32[17,16,128]{2,1,0:T(8,128)S(1)} %collective-permute-done.4.even), channel_id=1, source_target_pairs={{0,1},{1,0},{8,9},{9,8},{16,17},{17,16},{24,25},{25,24},{26,27},{2... | collective-permute-start | bytes 417800 | tf_op jit(solution)/shard_map/ppermute | solution.py:137
  28.5 4.7 %collective-permute-start.9 = (f32[17,16,128]{2,1,0:T(8,128)S(1)}, f32[17,16,128]{2,1,0:T(8,128)S(1)}, u32[]{:S(2)}, u32[]{:S(2)}) collective-permute-start(f32[17,16,128]{2,1,0:T(8,128)S(1)} %collective-permute-done.5.odd), channel_id=1, source_target_pairs={{0,1},{1,0},{8,9},{9,8},{16,17},{17,16},{24,25},{25,24},{26,27},{2... | collective-permute-start | bytes 417800 | tf_op jit(solution)/shard_map/ppermute | solution.py:137
  30.4 1.3 %collective-permute-start.10 = (f32[16,16,128]{2,1,0:T(8,128)S(1)}, f32[16,16,128]{2,1,0:T(8,128)S(1)}, u32[]{:S(2)}, u32[]{:S(2)}) collective-permute-start(f32[16,16,128]{2,1,0:T(8,128)S(1)} %collective-permute-done.2.even), channel_id=1, source_target_pairs={{0,1},{1,0},{8,9},{9,8},{16,17},{17,16},{24,25},{25,24},{26,27},{2... | collective-permute-start | bytes 393224 | tf_op jit(solution)/shard_map/ppermute | solution.py:137
  30.4 1.5 %collective-permute-start.11 = (f32[16,16,128]{2,1,0:T(8,128)S(1)}, f32[16,16,128]{2,1,0:T(8,128)S(1)}, u32[]{:S(2)}, u32[]{:S(2)}) collective-permute-start(f32[16,16,128]{2,1,0:T(8,128)S(1)} %collective-permute-done.3.odd), channel_id=1, source_target_pairs={{0,1},{1,0},{8,9},{9,8},{16,17},{17,16},{24,25},{25,24},{26,27},{2... | collective-permute-start | bytes 393224 | tf_op jit(solution)/shard_map/ppermute | solution.py:137
  35.1 5.9 %collective-permute-start.12 = (f32[32,16,128]{2,1,0:T(8,128)S(1)}, f32[32,16,128]{2,1,0:T(8,128)S(1)}, u32[]{:S(2)}, u32[]{:S(2)}) collective-permute-start(f32[32,16,128]{2,1,0:T(8,128)S(1)} %get-tuple-element.57.mine), channel_id=1, source_target_pairs={{0,5},{8,1},{16,9},{24,17},{26,25},{18,27},{10,19},{2,11},{6,3},{1... | collective-permute-start | bytes 786440 | tf_op jit(solution)/shard_map/ppermute | solution.py:157
  41.0 1.5 %collective-permute-start.13 = (f32[32,16,128]{2,1,0:T(8,128)S(1)}, f32[32,16,128]{2,1,0:T(8,128)S(1)}, u32[]{:S(2)}, u32[]{:S(2)}) collective-permute-start(f32[32,16,128]{2,1,0:T(8,128)S(1)} %collective-permute-done.12.side), channel_id=1, source_target_pairs={{0,1},{1,0},{8,9},{9,8},{16,17},{17,16},{24,25},{25,24},{26,27},{2... | collective-permute-start | bytes 786440 | tf_op jit(solution)/shard_map/ppermute | solution.py:137
  44.1 5.9 %collective-permute-start.14 = (f32[32,16,128]{2,1,0:T(8,128)S(1)}, f32[32,16,128]{2,1,0:T(8,128)S(1)}, u32[]{:S(2)}, u32[]{:S(2)}) collective-permute-start(f32[32,16,128]{2,1,0:T(8,128)S(1)} %get-tuple-element.62.mine), channel_id=1, source_target_pairs={{0,5},{8,1},{16,9},{24,17},{26,25},{18,27},{10,19},{2,11},{6,3},{1... | collective-permute-start | bytes 786440 | tf_op jit(solution)/shard_map/ppermute | solution.py:157
  50.0 1.5 %collective-permute-start.15 = (f32[32,16,128]{2,1,0:T(8,128)S(1)}, f32[32,16,128]{2,1,0:T(8,128)S(1)}, u32[]{:S(2)}, u32[]{:S(2)}) collective-permute-start(f32[32,16,128]{2,1,0:T(8,128)S(1)} %collective-permute-done.14.side), channel_id=1, source_target_pairs={{0,1},{1,0},{8,9},{9,8},{16,17},{17,16},{24,25},{25,24},{26,27},{2... | collective-permute-start | bytes 786440 | tf_op jit(solution)/shard_map/ppermute | solution.py:137
  70.4 1.7 %collective-permute-start.16 = (f32[3,4,32,128]{3,2,1,0:T(8,128)S(1)}, f32[3,4,32,128]{3,2,1,0:T(8,128)S(1)}, u32[]{:S(2)}, u32[]{:S(2)}) collective-permute-start(f32[3,4,32,128]{3,2,1,0:T(8,128)S(1)} %bitcast.14), channel_id=1, source_target_pairs={{0,1},{1,0},{8,9},{9,8},{16,17},{17,16},{24,25},{25,24},{26,27},{2... | collective-permute-start | bytes 589832 | tf_op jit(solution)/shard_map/ppermute | solution.py:137

commit v2 on v1

--- a/solution.py
+++ b/solution.py
@@ -246,17 +246,17 @@
     pl.when(c == 1)(lambda: write(recv_ref, keep_ref))
 
 
-def unpack_kernel(plan, in_ref, s_ref, t_ref):
+def unpack_kernel(plan, st, in_ref, out_ref):
     S, gs, XH = plan.S, plan.gs, plan.XH
     size = 2 * S + 1
-    for st, out_ref in enumerate((s_ref, t_ref)):
-        for i in range(plan.nx):
-            bases = [size * (i * plan.ny + j) + S * st for j in range(plan.ny)]
-            parts = [in_ref[base : base + S, :] for base in bases]
-            for xx, value in enumerate(turn_groups(plan, parts)):
-                out_ref[i * gs + xx] = value
-    t_ref[XH] = jnp.zeros((S, LANES), jnp.float32)
-    t_ref[XH, :1, :] = sum_rows(in_ref, size)
+    for i in range(plan.nx):
+        bases = [size * (i * plan.ny + j) + S * st for j in range(plan.ny)]
+        parts = [in_ref[base : base + S, :] for base in bases]
+        for xx, value in enumerate(turn_groups(plan, parts)):
+            out_ref[i * gs + xx] = value
+    if st:
+        out_ref[XH] = jnp.zeros((S, LANES), jnp.float32)
+        out_ref[XH, :1, :] = sum_rows(in_ref, size)
 
 
 def sum_rows(ref, size):
@@ -386,7 +386,8 @@
     ref[edge + size :] = blank
 
 
-def prep_kernel(plan, k_ref, s_ref, own, taps_ref, quad_ref, slope_ref, smooth_ref, high_ref, low_ref):
+def prep_kernel(plan, k_ref, s_ref, own, taps_ref, quad_ref, slope_ref, smooth_ref, high_ref,
+                low_ref, plane_ref, line_ref):
     del own
     R, Q = plan.R, plan.Q
     taps = [jnp.zeros((1, LANES), jnp.float32) + k_ref[d] for d in range(R + 1)]
@@ -403,6 +404,21 @@
     high_ref[...], low_ref[...] = halves(banded(wide, plan.Z, False))
 
 
+    def reach_sum(shape, axis, start, size):
+        place = lax.broadcasted_iota(jnp.int32, shape, axis) + start
+        total = jnp.ones(shape, jnp.float32)
+        for d in range(1, R + 1):
+            total = total + jnp.where(place - d >= 0, taps[d], 0.0)
+            total = total + jnp.where(place + d < size, taps[d], 0.0)
+        return total
+
+    at = place_of(plan)
+    shape = plane_ref.shape
+    over = reach_sum(shape, 0, at * plan.S - plan.H, plan.Z) * reach_sum(shape, 1, 0, plan.Y)
+    plane_ref[...] = jnp.where(inside(plan, at, 0, shape[0]), 1.0 / over, 0.0)
+    line_ref[...] = 1.0 / reach_sum(line_ref.shape, 0, 0, plan.X)
+
+
 def kernel_taps(plan, taps_ref):
     return [taps_ref[d, :1, :] for d in range(plan.R + 1)]
 
@@ -474,37 +490,21 @@
     pl.when(at % 2 == 1)(lambda: spread((even, even2), (odd, odd2)))
 
 
-def open_kernel(plan, taps_ref, quad_ref, own, even, odd, own2, even2, odd2, sw, ku, u, zb):
-    R, S, H, X = plan.R, plan.S, plan.H, plan.X
+def open_kernel(plan, taps_ref, quad_ref, plane_ref, line_ref, own, even, odd, own2, even2, odd2,
+                sw, ku, u, zb):
+    R = plan.R
     at = place_of(plan)
     taps = kernel_taps(plan, taps_ref)
-    clear_edges(zb, R, X)
+    clear_edges(zb, R, plan.X)
     spread_halves(plan, at, own, even, odd, own2, even2, odd2, sw)
-
-    def reach_sum(place, size):
-        total = jnp.ones(place.shape, jnp.float32)
-        for d in range(1, R + 1):
-            total = total + jnp.where(place - d >= 0, taps[d], 0.0)
-            total = total + jnp.where(place + d < size, taps[d], 0.0)
-        return total
-
-    rows = S + 2 * H
-    mask = inside(plan, at, 0, rows)
-    y_at = lax.broadcasted_iota(jnp.int32, (rows, LANES), 1)
-    z_at = lax.broadcasted_iota(jnp.int32, (rows, LANES), 0) + (at * S - H)
-    plane = reach_sum(z_at, plan.Z) * (reach_sum(y_at, plan.Y) * taps_ref[0, :1, :])
-
-    def u_step(x, carry):
-        cx = reach_sum(jnp.zeros((1, LANES), jnp.int32) + x, X)
-        u[x] = jnp.where(mask, sw[x] / (plane * cx), 0.0)
-        return carry
-
-    lax.fori_loop(0, X, u_step, 0, unroll=2)
+    for x in range(plan.X):
+        u[x] = sw[x] * (plane_ref[...] * line_ref[x : x + 1, :])
 
     def emit(x, value):
         ku[x] = value
 
-    run_passes(plan, [kernel_pass(plan, taps, quad_ref, u, zb, rows - 2 * R, emit)])
+    rows = ku.shape[1]
+    run_passes(plan, [kernel_pass(plan, taps, quad_ref, u, zb, rows, emit)])
 
 
 def first_kernel(plan, taps_ref, quad_ref, own, even, odd, own2, even2, odd2, sw, ku,
@@ -703,33 +703,41 @@
     smooth_z(plan, 1 - lax.axis_index("gz"), high_ref, low_ref, in_ref, data, emit)
 
 
-def home_kernel(plan, high_ref, low_ref, in_ref, mis_ref, out_hbm, data, keep, sem):
+def home_kernel(plan, high_ref, low_ref, in_ref, mis_ref, out_hbm, data, keep, sems):
     c = lax.axis_index("gz")
     gs = plan.gs
-
-    def emit(comp, value):
-        keep[comp] = value.reshape(gs, plan.by, LANES)
-
-    smooth_z(plan, c, high_ref, low_ref, in_ref, data, emit)
-    copy = pltpu.make_async_copy(keep, out_hbm.at[:, pl.ds(gs * c, gs)], sem)
-    copy.start()
     gone = sum_rows(in_ref, 3 * plan.S // 2 + 1) / plan.cells
     for t in range(ITERS):
         mis_ref[t] = jnp.sum(jnp.where(lane_at() == t, gone, 0.0))
-    copy.wait()
-
-
-def place_kernel(plan, recv_ref, in_hbm, out_hbm, sem):
+    copies = [
+        pltpu.make_async_copy(keep.at[k], out_hbm.at[k, pl.ds(gs * c, gs)], sems.at[k])
+        for k in range(3)
+    ]
+
+    def emit(comp, value):
+        keep[comp] = value.reshape(gs, plan.by, LANES)
+        copies[comp].start()
+
+    smooth_z(plan, c, high_ref, low_ref, in_ref, data, emit)
+    for copy in copies:
+        copy.wait()
+
+
+def place_kernel(plan, recv_ref, in_hbm, out_hbm, sems):
     del in_hbm
-    c = lax.axis_index("gz")
-    copy = pltpu.make_async_copy(recv_ref, out_hbm.at[:, pl.ds(plan.gs * (1 - c), plan.gs)], sem)
-    copy.start()
-    copy.wait()
+    at = pl.ds(plan.gs * (1 - lax.axis_index("gz")), plan.gs)
+    copies = [
+        pltpu.make_async_copy(recv_ref.at[k], out_hbm.at[k, at], sems.at[k]) for k in range(3)
+    ]
+    for copy in copies:
+        copy.start()
+    for copy in copies:
+        copy.wait()
 
 
 def slab_shards(plan, source, target, kernel_half, smooth_half):
     R, S, H, X, XH, Pn, Z = plan.R, plan.S, plan.H, plan.X, plan.XH, plan.P, plan.Z
-    bind = lambda kernel: functools.partial(kernel, plan)
+    bind = lambda kernel, *more: functools.partial(kernel, plan, *more)
     half = f32(2, LANES, LANES)
     vm = lambda *shape: pltpu.VMEM(shape, jnp.float32)
     keep, stat = call(
@@ -740,13 +748,15 @@
         bind(chunk_kernel), [f32(Pn * (2 * S + 1), LANES)], 0, 4, [vm(*half.shape)]
     )(keep, swap_cores(plan, source), swap_cores(plan, target), stat)
     spread = trade_chunks(chunks, ("gx", "gy"))
-    own_s, own_t = call(
-        bind(unpack_kernel), [f32(XH, S, LANES), f32(XH + 1, S, LANES)], 0, 1
-    )(spread)
+    unpack = lambda st: call(bind(unpack_kernel, st), [f32(XH + st, S, LANES)], 0, 1)(spread)[0]
+    own_s = unpack(0)
+    own_t = unpack(1)
     square = jax.ShapeDtypeStruct((2 * LANES, 2 * LANES), jnp.bfloat16)
     table = jax.ShapeDtypeStruct((Z, Z), jnp.bfloat16)
-    taps, quad_k, quad_g, quad_s, high, low = call(
-        bind(prep_kernel), [f32(plan.R + plan.Q + 2, 8, LANES), square, square, square, table, table],
+    taps, quad_k, quad_g, quad_s, high, low, plane, line = call(
+        bind(prep_kernel),
+        [f32(R + plan.Q + 2, 8, LANES), square, square, square, table, table,
+         f32(S + 2 * H, LANES), f32(X, LANES)],
         2, 0, n_any=1,
     )(kernel_half, smooth_half, own_s)
     even_s, odd_s = swap_even(plan, own_s), swap_odd(plan, own_s)
@@ -762,8 +772,8 @@
     wide, v_shape, u_shape, v2_shape = (f32(X, width - 2 * k * R, LANES) for k in (0, 1, 2, 3))
     zb = vm(X + 2 * R, width - 2 * R, LANES)
     sw, ku = call(
-        bind(open_kernel), [wide, v_shape], 0, 8, [vm(*wide.shape), zb]
-    )(taps, quad_k, own_s, even_s, odd_s, own2_s, *halos_s)
+        bind(open_kernel), [wide, v_shape], 0, 10, [vm(*wide.shape), zb]
+    )(taps, quad_k, plane, line, own_s, even_s, odd_s, own2_s, *halos_s)
     tw, v1, v2, u, tot = call(
         bind(first_kernel), [wide, v_shape, v2_shape, slab, f32(1, LANES)], 0, 10,
         [vm(*u_shape.shape), zb, zb],
@@ -800,11 +810,11 @@
     recv = swap_cores(plan, send.reshape(half))
     whole = f32(3, plan.bx, plan.by, LANES)
     mismatch, displacement = call(
-        bind(home_kernel), [f32(ITERS), whole], 0, 3, [data, vm(*half), pltpu.SemaphoreType.DMA(())],
+        bind(home_kernel), [f32(ITERS), whole], 0, 3, [data, vm(*half), pltpu.SemaphoreType.DMA((3,))],
         smem_out=1, any_out=1,
     )(high, low, spread)
     (displacement,) = call(
-        bind(place_kernel), [whole], 0, 1, [pltpu.SemaphoreType.DMA(())], n_any=1, any_out=1,
+        bind(place_kernel), [whole], 0, 1, [pltpu.SemaphoreType.DMA((3,))], n_any=1, any_out=1,
         aliases={1: 0},
     )(recv, displacement)
     return displacement, mismatch

time: 73 us -> 72.6 us (level)
    pallas_call x4 -> x5, Pallas kernels: 3.02 us -> 2.87 us  [the longest x1 1.01 us: slab_shards(): call(bind(open_kernel), [wide, v_shape], 0, 10, [vm(*wide.shape), zb])]
where the time goes in v2:
time: 72.6 us; the launch traced here: 72.4 us
  blocking collectives  34.8 us (48%)
  Pallas kernels  14.3 us (20%)
  waiting for transfers between devices  14.2 us (20%)
  starting transfers between devices  8.2 us (11%)
  between operations  0.83 us (1%)
    all_to_all x2, blocking collectives, trade_chunks(): out = lax.all_to_all(value.reshape(rows, 1, lanes), axes, 0, 0, tiled=True)  34.8 us
    ppermute x2, waiting for transfers between devices, swap_sides(): return lax.ppermute(value, AXES, pairs)  9.13 us
    ppermute x11, starting transfers between devices, swap_cores(): return lax.ppermute(value, AXES, pairs)  2.45 us
    pallas_call x2, Pallas kernels, early(): call(bind(early_kernel), [v_shape, u_shape, v2_shape], 0, 6, [vm(X, S + H...  2.32 us
    ppermute x2, starting transfers between devices, swap_sides(): return lax.ppermute(value, AXES, pairs)  2.19 us
    pallas_call x1, Pallas kernels, slab_shards(): call(bind(last_kernel), [v_shape, u_shape, v2_shape, f32(2 * Pn * (3 * S...  2.09 us
    ppermute x2, starting transfers between devices, swap_odd(): return lax.ppermute(value, AXES, pairs)  2.06 us
    pallas_call x1, Pallas kernels, slab_shards(): call(bind(first_kernel), [wide, v_shape, v2_shape, slab, f32(1, LANES)],...  1.89 us
  transfers between devices with their start and end apart: 17, of which 8 were waited for; matrix products, arithmetic and copies ran while one was open for 0% of the time, Pallas kernels for 10%

profile of v2, /device:TPU:0, one launch (start us, length us, event | category | flops | bytes accessed | tf_op | source)
XLA Modules:
  0.0 72.4 jit_solution(11287246589679171280)
XLA Ops:
  0.6 0.6 collective-permute-start
  1.2 0.1 collective-permute-start.1
  1.3 1.2 %shard_map.59 = (f32[2,128,128]{2,1,0:T(8,128)S(1)}, f32[1,128]{1,0:T(1,128)S(1)}) custom-call(f32[8,32,128]{2,1,0:T(8,128)} %src_hbm.1, f32[8,32,128]{2,1,0:T(8,128)} %tgt_hbm.1), custom_call_target="tpu_custom_call" | custom-call | tf_op jit(solution)/shard_map/pallas_call | solution.py:743
  2.5 0.0 collective-permute-done.src_ref
  2.5 0.3 collective-permute-done.1.tgt_ref
  2.7 0.1 shard_map.60
  2.9 18.4 %all_to_all.10 = f32[528,1,128]{2,1,0:T(1,128)S(1)} all-to-all(f32[528,1,128]{2,1,0:T(1,128)S(1)} %bitcast.13), channel_id=1, replica_groups=mesh['gx'=4,'gy'=4,'gz'=2] {'gx','gy'}, dimensions={0} | all-to-all | bytes 540672 | tf_op jit(solution)/shard_map/all_to_all | solution.py:162
  21.2 0.2 shard_map.63.own
  21.4 0.0 copy-start
  21.4 0.0 copy-start.1
  21.4 1.0 %collective-permute-start.5 = (f32[17,16,128]{2,1,0:T(8,128)S(1)}, f32[17,16,128]{2,1,0:T(8,128)S(1)}, u32[]{:S(2)}, u32[]{:S(2)}) collective-permute-start(f32[17,16,128]{2,1,0:T(8,128)S(1)} %shard_map.63.own), channel_id=1, source_target_pairs={{0,4},{1,5},{8,16},{9,17},{16,8},{17,9},{24,26},{25,27},{26,24},{2... | collective-permute-start | bytes 417800 | tf_op jit(solution)/shard_map/ppermute | solution.py:151
  22.4 0.3 collective-permute-start.4
  22.7 0.2 shard_map.61.own
  22.8 0.1 collective-permute-start.6
  22.9 1.1 %collective-permute-start.3 = (f32[16,16,128]{2,1,0:T(8,128)S(1)}, f32[16,16,128]{2,1,0:T(8,128)S(1)}, u32[]{:S(2)}, u32[]{:S(2)}) collective-permute-start(f32[16,16,128]{2,1,0:T(8,128)S(1)} %shard_map.61.own), channel_id=1, source_target_pairs={{0,4},{1,5},{8,16},{9,17},{16,8},{17,9},{24,26},{25,27},{26,24},{2... | collective-permute-start | bytes 393224 | tf_op jit(solution)/shard_map/ppermute | solution.py:151
  24.0 1.2 %collective-permute-start.2 = (f32[16,16,128]{2,1,0:T(8,128)S(1)}, f32[16,16,128]{2,1,0:T(8,128)S(1)}, u32[]{:S(2)}, u32[]{:S(2)}) collective-permute-start(f32[16,16,128]{2,1,0:T(8,128)S(1)} %shard_map.61.own), channel_id=1, source_target_pairs={{0,8},{1,9},{8,0},{9,1},{16,24},{17,25},{24,16},{25,17},{26,18},{2... | collective-permute-start | bytes 393224 | tf_op jit(solution)/shard_map/ppermute | solution.py:142
  25.2 0.0 collective-permute-done.6.own2
  25.2 0.0 collective-permute-start.7
  25.2 1.8 %collective-permute-done.5.odd = f32[17,16,128]{2,1,0:T(8,128)S(1)} collective-permute-done((f32[17,16,128]{2,1,0:T(8,128)S(1)}, f32[17,16,128]{2,1,0:T(8,128)S(1)}, u32[]{:S(2)}, u32[]{:S(2)}) %collective-permute-start.5) | collective-permute-done | bytes 139296 | tf_op jit(solution)/shard_map/ppermute | solution.py:151
  27.1 1.1 %collective-permute-done.4.even = f32[17,16,128]{2,1,0:T(8,128)S(1)} collective-permute-done((f32[17,16,128]{2,1,0:T(8,128)S(1)}, f32[17,16,128]{2,1,0:T(8,128)S(1)}, u32[]{:S(2)}, u32[]{:S(2)}) %collective-permute-start.4) | collective-permute-done | bytes 139296 | tf_op jit(solution)/shard_map/ppermute | solution.py:142
  28.2 0.0 collective-permute-start.8
  28.2 0.5 collective-permute-start.9
  28.7 0.0 copy-done
  28.7 0.0 copy-done.1
  28.7 0.8 %shard_map.62 = (f32[14,8,128]{2,1,0:T(8,128)S(1)}, bf16[256,256]{1,0:T(8,128)(2,1)S(1)}, bf16[256,256]{1,0:T(8,128)(2,1)S(1)}, bf16[256,256]{1,0:T(8,128)(2,1)S...) custom-call(f32[5]{0:T(128)S(1)} %copy-done, ...), custom_call_target="tpu_custom_call" | custom-call | tf_op jit(solution)/shard_map/pallas_call | solution.py:756
  29.5 0.0 collective-permute-done.3.odd
  29.6 0.7 %collective-permute-done.2.even = f32[16,16,128]{2,1,0:T(8,128)S(1)} collective-permute-done((f32[16,16,128]{2,1,0:T(8,128)S(1)}, f32[16,16,128]{2,1,0:T(8,128)S(1)}, u32[]{:S(2)}, u32[]{:S(2)}) %collective-permute-start.2) | collective-permute-done | bytes 131104 | tf_op jit(solution)/shard_map/ppermute | solution.py:142
  30.3 0.0 collective-permute-start.10
  30.3 0.5 collective-permute-start.11
  30.8 0.8 %collective-permute-done.10.even2 = f32[16,16,128]{2,1,0:T(8,128)S(1)} collective-permute-done((f32[16,16,128]{2,1,0:T(8,128)S(1)}, f32[16,16,128]{2,1,0:T(8,128)S(1)}, u32[]{:S(2)}, u32[]{:S(2)}) %collective-permute-start.10) | collective-permute-done | bytes 131104 | tf_op jit(solution)/shard_map/ppermute | solution.py:137
  31.6 0.2 collective-permute-done.11.odd2
  31.8 1.0 %shard_map.64 = (f32[32,48,128]{2,1,0:T(8,128)S(1)}, f32[32,40,128]{2,1,0:T(8,128)S(1)}) custom-call(f32[14,8,128]{2,1,0:T(8,128)S(1)} %get-tuple-element.44.taps_ref, bf16[256,256]{1,0:T(8,128)(2,1)S(1)} %get-tuple-element.45.quad_ref, f32[48,128]{1,0:T(8,128)S(1)} %get-tuple-element.50.plane_ref, f32[32,128]{1,0:T(8,128)S(1)} %get-tuple-element.51.line_ref, ...), custom_call_target="tpu_custom_call" | custom-call | tf_op jit(solution)/shard_map/pallas_call | solution.py:774
  32.8 0.0 collective-permute-done.7.own2
  32.8 0.0 collective-permute-done.8.even2
  32.8 0.0 collective-permute-done.9.odd2
  32.9 1.9 %shard_map.65 = (f32[32,48,128]{2,1,0:T(8,128)S(1)}, f32[32,40,128]{2,1,0:T(8,128)S(1)}, f32[32,24,128]{2,1,0:T(8,128)S(1)}, f32[32,16,128]{2,1,0:T(8,128)S(1)}, f32[1,128]{1,0:T(1,128)S(1)}) custom-call(f32[14,8,128]{2,1,0:T(8,128)S(1)} %get-tuple-element.44.taps_ref, bf16[256,256]{1,0:T(8,128)(2,1)S(1)} %get-tuple-element.45.quad_ref, ...), custom_call_target="tpu_custom_call" | custom-call | tf_op jit(solution)/shard_map/pallas_call | solution.py:777
  34.8 1.1 %collective-permute-start.12 = (f32[32,16,128]{2,1,0:T(8,128)S(1)}, f32[32,16,128]{2,1,0:T(8,128)S(1)}, u32[]{:S(2)}, u32[]{:S(2)}) collective-permute-start(f32[32,16,128]{2,1,0:T(8,128)S(1)} %get-tuple-element.57.mine), channel_id=1, source_target_pairs={{0,5},{8,1},{16,9},{24,17},{26,25},{18,27},{10,19},{2,11},{6,3},{1... | collective-permute-start | bytes 786440 | tf_op jit(solution)/shard_map/ppermute | solution.py:157
  35.9 4.8 %collective-permute-done.12.side = f32[32,16,128]{2,1,0:T(8,128)S(1)} collective-permute-done((f32[32,16,128]{2,1,0:T(8,128)S(1)}, f32[32,16,128]{2,1,0:T(8,128)S(1)}, u32[]{:S(2)}, u32[]{:S(2)}) %collective-permute-start.12) | collective-permute-done | bytes 262176 | tf_op jit(solution)/shard_map/ppermute | solution.py:157
  40.6 0.3 collective-permute-start.13
  40.9 1.2 %shard_map.66 = (f32[32,40,128]{2,1,0:T(8,128)S(1)}, f32[32,32,128]{2,1,0:T(8,128)S(1)}, f32[32,24,128]{2,1,0:T(8,128)S(1)}) custom-call(f32[14,8,128]{2,1,0:T(8,128)S(1)} %get-tuple-element.44.taps_ref, bf16[256,256]{1,0:T(8,128)(2,1)S(1)} %get-tuple-element.45.quad_ref, f32[32,16,128]{2,1,0:T(8,128)S(1)} %get-tuple-element.57.mine, ...), custom_call_target="tpu_custom_call" | custom-call | tf_op jit(solution)/shard_map/pallas_call | solution.py:783
  42.1 0.0 collective-permute-done.13.other
  42.2 1.6 %shard_map.67 = (f32[32,40,128]{2,1,0:T(8,128)S(1)}, f32[32,32,128]{2,1,0:T(8,128)S(1)}, f32[32,24,128]{2,1,0:T(8,128)S(1)}, f32[32,16,128]{2,1,0:T(8,128)S(1)}) custom-call(f32[14,8,128]{2,1,0:T(8,128)S(1)} %get-tuple-element.44.taps_ref, ...), custom_call_target="tpu_custom_call", output_to_operand_aliasing={{0}: (6, {}), {1}: (7, {}), {2}: (8, {})} | custom-call | tf_op jit(solution)/shard_map/pallas_call | solution.py:792
  43.7 1.1 %collective-permute-start.14 = (f32[32,16,128]{2,1,0:T(8,128)S(1)}, f32[32,16,128]{2,1,0:T(8,128)S(1)}, u32[]{:S(2)}, u32[]{:S(2)}) collective-permute-start(f32[32,16,128]{2,1,0:T(8,128)S(1)} %get-tuple-element.62.mine), channel_id=1, source_target_pairs={{0,5},{8,1},{16,9},{24,17},{26,25},{18,27},{10,19},{2,11},{6,3},{1... | collective-permute-start | bytes 786440 | tf_op jit(solution)/shard_map/ppermute | solution.py:157
  44.8 0.4 shard_map.68.gaps
  45.2 4.4 %collective-permute-done.14.side = f32[32,16,128]{2,1,0:T(8,128)S(1)} collective-permute-done((f32[32,16,128]{2,1,0:T(8,128)S(1)}, f32[32,16,128]{2,1,0:T(8,128)S(1)}, u32[]{:S(2)}, u32[]{:S(2)}) %collective-permute-start.14) | collective-permute-done | bytes 262176 | tf_op jit(solution)/shard_map/ppermute | solution.py:157
  49.6 0.3 collective-permute-start.15
  49.9 1.2 %shard_map.69 = (f32[32,40,128]{2,1,0:T(8,128)S(1)}, f32[32,32,128]{2,1,0:T(8,128)S(1)}, f32[32,24,128]{2,1,0:T(8,128)S(1)}) custom-call(f32[14,8,128]{2,1,0:T(8,128)S(1)} %get-tuple-element.44.taps_ref, bf16[256,256]{1,0:T(8,128)(2,1)S(1)} %get-tuple-element.45.quad_ref, f32[32,16,128]{2,1,0:T(8,128)S(1)} %get-tuple-element.62.mine, ...), custom_call_target="tpu_custom_call" | custom-call | tf_op jit(solution)/shard_map/pallas_call | solution.py:783
  51.1 0.0 collective-permute-done.15.other
  51.1 2.1 %shard_map.70 = (f32[32,40,128]{2,1,0:T(8,128)S(1)}, f32[32,32,128]{2,1,0:T(8,128)S(1)}, f32[32,24,128]{2,1,0:T(8,128)S(1)}, f32[800,128]{1,0:T(8,128)S(1)}) custom-call(f32[14,8,128]{2,1,0:T(8,128)S(1)} %get-tuple-element.44.taps_ref, ...), custom_call_target="tpu_custom_call", output_to_operand_aliasing={{0}: (11, {}), {1}: (12, {}), {2}: (13, {})} | custom-call | tf_op jit(solution)/shard_map/pallas_call | solution.py:801
  53.2 16.5 %all_to_all.11 = f32[800,1,128]{2,1,0:T(1,128)S(1)} all-to-all(f32[800,1,128]{2,1,0:T(1,128)S(1)} %bitcast.14), channel_id=1, replica_groups=mesh['gx'=4,'gy'=4,'gz'=2] {'gx','gy','gz'}, dimensions={0} | all-to-all | bytes 819200 | tf_op jit(solution)/shard_map/all_to_all | solution.py:162
  69.7 0.4 shard_map.71
  70.0 0.1 collective-permute-start.16
  70.1 1.6 %shard_map.72 = (f32[6]{0:T(128)}, f32[3,8,32,128]{3,2,1,0:T(8,128)}) custom-call(bf16[256,256]{1,0:T(8,128)(2,1)S(1)} %get-tuple-element.41.high_ref, bf16[256,256]{1,0:T(8,128)(2,1)S(1)} %get-tuple-element.42.low_ref, f32[800,128]{1,0:T(8,128)S(1)} %bitcast.10), custom_call_target="tpu_custom_call" | custom-call | tf_op jit(solution)/shard_map/pallas_call | solution.py:812
  71.7 0.0 collective-permute-done.16.recv_ref
  71.7 0.7 shard_map.73
Async XLA Ops:
  0.6 1.8 %collective-permute-start = (f32[8,32,128]{2,1,0:T(8,128)}, f32[8,32,128]{2,1,0:T(8,128)S(1)}, u32[]{:S(2)}, u32[]{:S(2)}) collective-permute-start(f32[8,32,128]{2,1,0:T(8,128)} %src_hbm.1), channel_id=1, source_target_pairs={{0,1},{1,0},{8,9},{9,8},{16,17},{17,16},{24,25},{25,24},{26,27},{2... | collective-permute-start | bytes 393224 | tf_op jit(solution)/shard_map/ppermute | solution.py:137
  1.2 1.6 %collective-permute-start.1 = (f32[8,32,128]{2,1,0:T(8,128)}, f32[8,32,128]{2,1,0:T(8,128)S(1)}, u32[]{:S(2)}, u32[]{:S(2)}) collective-permute-start(f32[8,32,128]{2,1,0:T(8,128)} %tgt_hbm.1), channel_id=1, source_target_pairs={{0,1},{1,0},{8,9},{9,8},{16,17},{17,16},{24,25},{25,24},{26,27},{2... | collective-permute-start | bytes 393224 | tf_op jit(solution)/shard_map/ppermute | solution.py:137
  21.4 7.3 %copy-start = (f32[5]{0:T(128)S(1)}, f32[5]{0:T(128)}, u32[]{:S(2)}) copy-start(f32[5]{0:T(128)} %k_ref.1) | copy-start | bytes 64
  21.4 7.3 %copy-start.1 = (f32[9]{0:T(128)S(1)}, f32[9]{0:T(128)}, u32[]{:S(2)}) copy-start(f32[9]{0:T(128)} %s_ref.1) | copy-start | bytes 112
  21.4 5.6 %collective-permute-start.5 = (f32[17,16,128]{2,1,0:T(8,128)S(1)}, f32[17,16,128]{2,1,0:T(8,128)S(1)}, u32[]{:S(2)}, u32[]{:S(2)}) collective-permute-start(f32[17,16,128]{2,1,0:T(8,128)S(1)} %shard_map.63.own), channel_id=1, source_target_pairs={{0,4},{1,5},{8,16},{9,17},{16,8},{17,9},{24,26},{25,27},{26,24},{2... | collective-permute-start | bytes 417800 | tf_op jit(solution)/shard_map/ppermute | solution.py:151
  22.4 5.8 %collective-permute-start.4 = (f32[17,16,128]{2,1,0:T(8,128)S(1)}, f32[17,16,128]{2,1,0:T(8,128)S(1)}, u32[]{:S(2)}, u32[]{:S(2)}) collective-permute-start(f32[17,16,128]{2,1,0:T(8,128)S(1)} %shard_map.63.own), channel_id=1, source_target_pairs={{0,8},{1,9},{8,0},{9,1},{16,24},{17,25},{24,16},{25,17},{26,18},{2... | collective-permute-start | bytes 417800 | tf_op jit(solution)/shard_map/ppermute | solution.py:142
  22.8 2.4 %collective-permute-start.6 = (f32[16,16,128]{2,1,0:T(8,128)S(1)}, f32[16,16,128]{2,1,0:T(8,128)S(1)}, u32[]{:S(2)}, u32[]{:S(2)}) collective-permute-start(f32[16,16,128]{2,1,0:T(8,128)S(1)} %shard_map.61.own), channel_id=1, source_target_pairs={{0,1},{1,0},{8,9},{9,8},{16,17},{17,16},{24,25},{25,24},{26,27},{2... | collective-permute-start | bytes 393224 | tf_op jit(solution)/shard_map/ppermute | solution.py:137
  22.9 6.6 %collective-permute-start.3 = (f32[16,16,128]{2,1,0:T(8,128)S(1)}, f32[16,16,128]{2,1,0:T(8,128)S(1)}, u32[]{:S(2)}, u32[]{:S(2)}) collective-permute-start(f32[16,16,128]{2,1,0:T(8,128)S(1)} %shard_map.61.own), channel_id=1, source_target_pairs={{0,4},{1,5},{8,16},{9,17},{16,8},{17,9},{24,26},{25,27},{26,24},{2... | collective-permute-start | bytes 393224 | tf_op jit(solution)/shard_map/ppermute | solution.py:151
  24.0 6.3 %collective-permute-start.2 = (f32[16,16,128]{2,1,0:T(8,128)S(1)}, f32[16,16,128]{2,1,0:T(8,128)S(1)}, u32[]{:S(2)}, u32[]{:S(2)}) collective-permute-start(f32[16,16,128]{2,1,0:T(8,128)S(1)} %shard_map.61.own), channel_id=1, source_target_pairs={{0,8},{1,9},{8,0},{9,1},{16,24},{17,25},{24,16},{25,17},{26,18},{2... | collective-permute-start | bytes 393224 | tf_op jit(solution)/shard_map/ppermute | solution.py:142
  25.2 7.6 %collective-permute-start.7 = (f32[17,16,128]{2,1,0:T(8,128)S(1)}, f32[17,16,128]{2,1,0:T(8,128)S(1)}, u32[]{:S(2)}, u32[]{:S(2)}) collective-permute-start(f32[17,16,128]{2,1,0:T(8,128)S(1)} %shard_map.63.own), channel_id=1, source_target_pairs={{0,1},{1,0},{8,9},{9,8},{16,17},{17,16},{24,25},{25,24},{26,27},{2... | collective-permute-start | bytes 417800 | tf_op jit(solution)/shard_map/ppermute | solution.py:137
  28.2 4.6 %collective-permute-start.8 = (f32[17,16,128]{2,1,0:T(8,128)S(1)}, f32[17,16,128]{2,1,0:T(8,128)S(1)}, u32[]{:S(2)}, u32[]{:S(2)}) collective-permute-start(f32[17,16,128]{2,1,0:T(8,128)S(1)} %collective-permute-done.4.even), channel_id=1, source_target_pairs={{0,1},{1,0},{8,9},{9,8},{16,17},{17,16},{24,25},{25,24},{26,27},{2... | collective-permute-start | bytes 417800 | tf_op jit(solution)/shard_map/ppermute | solution.py:137
  28.2 4.7 %collective-permute-start.9 = (f32[17,16,128]{2,1,0:T(8,128)S(1)}, f32[17,16,128]{2,1,0:T(8,128)S(1)}, u32[]{:S(2)}, u32[]{:S(2)}) collective-permute-start(f32[17,16,128]{2,1,0:T(8,128)S(1)} %collective-permute-done.5.odd), channel_id=1, source_target_pairs={{0,1},{1,0},{8,9},{9,8},{16,17},{17,16},{24,25},{25,24},{26,27},{2... | collective-permute-start | bytes 417800 | tf_op jit(solution)/shard_map/ppermute | solution.py:137
  30.3 1.3 %collective-permute-start.10 = (f32[16,16,128]{2,1,0:T(8,128)S(1)}, f32[16,16,128]{2,1,0:T(8,128)S(1)}, u32[]{:S(2)}, u32[]{:S(2)}) collective-permute-start(f32[16,16,128]{2,1,0:T(8,128)S(1)} %collective-permute-done.2.even), channel_id=1, source_target_pairs={{0,1},{1,0},{8,9},{9,8},{16,17},{17,16},{24,25},{25,24},{26,27},{2... | collective-permute-start | bytes 393224 | tf_op jit(solution)/shard_map/ppermute | solution.py:137
  30.3 1.5 %collective-permute-start.11 = (f32[16,16,128]{2,1,0:T(8,128)S(1)}, f32[16,16,128]{2,1,0:T(8,128)S(1)}, u32[]{:S(2)}, u32[]{:S(2)}) collective-permute-start(f32[16,16,128]{2,1,0:T(8,128)S(1)} %collective-permute-done.3.odd), channel_id=1, source_target_pairs={{0,1},{1,0},{8,9},{9,8},{16,17},{17,16},{24,25},{25,24},{26,27},{2... | collective-permute-start | bytes 393224 | tf_op jit(solution)/shard_map/ppermute | solution.py:137
  34.8 5.9 %collective-permute-start.12 = (f32[32,16,128]{2,1,0:T(8,128)S(1)}, f32[32,16,128]{2,1,0:T(8,128)S(1)}, u32[]{:S(2)}, u32[]{:S(2)}) collective-permute-start(f32[32,16,128]{2,1,0:T(8,128)S(1)} %get-tuple-element.57.mine), channel_id=1, source_target_pairs={{0,5},{8,1},{16,9},{24,17},{26,25},{18,27},{10,19},{2,11},{6,3},{1... | collective-permute-start | bytes 786440 | tf_op jit(solution)/shard_map/ppermute | solution.py:157
  40.6 1.5 %collective-permute-start.13 = (f32[32,16,128]{2,1,0:T(8,128)S(1)}, f32[32,16,128]{2,1,0:T(8,128)S(1)}, u32[]{:S(2)}, u32[]{:S(2)}) collective-permute-start(f32[32,16,128]{2,1,0:T(8,128)S(1)} %collective-permute-done.12.side), channel_id=1, source_target_pairs={{0,1},{1,0},{8,9},{9,8},{16,17},{17,16},{24,25},{25,24},{26,27},{2... | collective-permute-start | bytes 786440 | tf_op jit(solution)/shard_map/ppermute | solution.py:137
  43.7 5.9 %collective-permute-start.14 = (f32[32,16,128]{2,1,0:T(8,128)S(1)}, f32[32,16,128]{2,1,0:T(8,128)S(1)}, u32[]{:S(2)}, u32[]{:S(2)}) collective-permute-start(f32[32,16,128]{2,1,0:T(8,128)S(1)} %get-tuple-element.62.mine), channel_id=1, source_target_pairs={{0,5},{8,1},{16,9},{24,17},{26,25},{18,27},{10,19},{2,11},{6,3},{1... | collective-permute-start | bytes 786440 | tf_op jit(solution)/shard_map/ppermute | solution.py:157
  49.6 1.5 %collective-permute-start.15 = (f32[32,16,128]{2,1,0:T(8,128)S(1)}, f32[32,16,128]{2,1,0:T(8,128)S(1)}, u32[]{:S(2)}, u32[]{:S(2)}) collective-permute-start(f32[32,16,128]{2,1,0:T(8,128)S(1)} %collective-permute-done.14.side), channel_id=1, source_target_pairs={{0,1},{1,0},{8,9},{9,8},{16,17},{17,16},{24,25},{25,24},{26,27},{2... | collective-permute-start | bytes 786440 | tf_op jit(solution)/shard_map/ppermute | solution.py:137
  70.0 1.6 %collective-permute-start.16 = (f32[3,4,32,128]{3,2,1,0:T(8,128)S(1)}, f32[3,4,32,128]{3,2,1,0:T(8,128)S(1)}, u32[]{:S(2)}, u32[]{:S(2)}) collective-permute-start(f32[3,4,32,128]{3,2,1,0:T(8,128)S(1)} %bitcast.15), channel_id=1, source_target_pairs={{0,1},{1,0},{8,9},{9,8},{16,17},{17,16},{24,25},{25,24},{26,27},{2... | collective-permute-start | bytes 589832 | tf_op jit(solution)/shard_map/ppermute | solution.py:137

commit v3 on v2

--- a/solution.py
+++ b/solution.py
@@ -678,37 +678,36 @@
         out_ref[size * (p + 1) - 1 : size * (p + 1), :] = stat
 
 
-def smooth_z(plan, core, high_ref, low_ref, in_ref, data, emit):
+def smooth_z(core, high_ref, low_ref, d_high, d_low, emit):
+    rows = pl.ds(pl.multiple_of(core * LANES, LANES), LANES)
+    m_high, m_low = high_ref[rows, :], low_ref[rows, :]
+    dot = functools.partial(jnp.dot, preferred_element_type=jnp.float32)
+    for comp in range(3):
+        lanes = slice(comp * LANES, (comp + 1) * LANES)
+        high, low = d_high[:, lanes], d_low[:, lanes]
+        emit(comp, (dot(m_high, high) + (dot(m_high, low) + dot(m_low, high))).T)
+
+
+def away_kernel(plan, high_ref, low_ref, in_ref, send_ref, d_high, d_low):
     half = plan.S // 2
     size = 3 * half + 1
-    for part in range(2 * plan.P):
-        for comp in range(3):
-            base = size * plan.device(part // 2, part % 2) + comp * half
-            data[half * part : half * (part + 1), comp * LANES : (comp + 1) * LANES] = in_ref[
-                base : base + half, :
-            ]
-    rows = pl.ds(pl.multiple_of(core * LANES, LANES), LANES)
-    m_high, m_low = high_ref[rows, :], low_ref[rows, :]
-    d_high, d_low = halves(data[...])
-    dot = functools.partial(jnp.dot, preferred_element_type=jnp.float32)
-    out = dot(m_high, d_high) + (dot(m_high, d_low) + dot(m_low, d_high))
     for comp in range(3):
-        emit(comp, out[:, comp * LANES : (comp + 1) * LANES].T)
-
-
-def away_kernel(plan, high_ref, low_ref, in_ref, send_ref, data):
+        for place in range(plan.P):
+            bases = [size * plan.device(place, core) + comp * half for core in range(2)]
+            both = jnp.concatenate([in_ref[base : base + half, :] for base in bases], axis=0)
+            here = slice(plan.S * place, plan.S * (place + 1))
+            lanes = slice(comp * LANES, (comp + 1) * LANES)
+            d_high[here, lanes], d_low[here, lanes] = halves(both)
+
     def emit(comp, value):
         send_ref[comp] = value
 
-    smooth_z(plan, 1 - lax.axis_index("gz"), high_ref, low_ref, in_ref, data, emit)
-
-
-def home_kernel(plan, high_ref, low_ref, in_ref, mis_ref, out_hbm, data, keep, sems):
+    smooth_z(1 - lax.axis_index("gz"), high_ref, low_ref, d_high, d_low, emit)
+
+
+def home_kernel(plan, high_ref, low_ref, d_high, d_low, in_ref, mis_ref, out_hbm, keep, sems):
     c = lax.axis_index("gz")
     gs = plan.gs
-    gone = sum_rows(in_ref, 3 * plan.S // 2 + 1) / plan.cells
-    for t in range(ITERS):
-        mis_ref[t] = jnp.sum(jnp.where(lane_at() == t, gone, 0.0))
     copies = [
         pltpu.make_async_copy(keep.at[k], out_hbm.at[k, pl.ds(gs * c, gs)], sems.at[k])
         for k in range(3)
@@ -718,7 +717,10 @@
         keep[comp] = value.reshape(gs, plan.by, LANES)
         copies[comp].start()
 
-    smooth_z(plan, c, high_ref, low_ref, in_ref, data, emit)
+    smooth_z(c, high_ref, low_ref, d_high, d_low, emit)
+    gone = sum_rows(in_ref, 3 * plan.S // 2 + 1) / plan.cells
+    for t in range(ITERS):
+        mis_ref[t] = jnp.sum(jnp.where(lane_at() == t, gone, 0.0))
     for copy in copies:
         copy.wait()
 
@@ -804,15 +806,17 @@
         aliases={11: 0, 12: 1, 13: 2},
     )(taps, quad_k, quad_g, quad_s, u, other, sw, tw, v4, gaps, tot, v5, u6, v6)
     spread = trade_chunks(chunks, AXES)
-    data = vm(Z, 3 * LANES)
-    (send,) = call(bind(away_kernel), [f32(3, LANES, LANES)], 0, 3, [data])(high, low, spread)
+    split = jax.ShapeDtypeStruct((Z, 3 * LANES), jnp.bfloat16)
+    send, *splits = call(
+        bind(away_kernel), [f32(3, LANES, LANES), split, split], 0, 3
+    )(high, low, spread)
     half = (3, plan.gs, plan.by, LANES)
     recv = swap_cores(plan, send.reshape(half))
     whole = f32(3, plan.bx, plan.by, LANES)
     mismatch, displacement = call(
-        bind(home_kernel), [f32(ITERS), whole], 0, 3, [data, vm(*half), pltpu.SemaphoreType.DMA((3,))],
+        bind(home_kernel), [f32(ITERS), whole], 0, 5, [vm(*half), pltpu.SemaphoreType.DMA((3,))],
         smem_out=1, any_out=1,
-    )(high, low, spread)
+    )(high, low, *splits, spread)
     (displacement,) = call(
         bind(place_kernel), [whole], 0, 1, [pltpu.SemaphoreType.DMA((3,))], n_any=1, any_out=1,
         aliases={1: 0},

time: 72.6 us -> 72.7 us (level)
  no operation moved by 1% of the time
where the time goes in v3:
time: 72.7 us; the launch traced here: 72.5 us
  blocking collectives  34.8 us (48%)
  Pallas kernels  14.4 us (20%)
  waiting for transfers between devices  14.2 us (20%)
  starting transfers between devices  8.2 us (11%)
  between operations  0.83 us (1%)
    all_to_all x2, blocking collectives, trade_chunks(): out = lax.all_to_all(value.reshape(rows, 1, lanes), axes, 0, 0, tiled=True)  34.8 us
    ppermute x2, waiting for transfers between devices, swap_sides(): return lax.ppermute(value, AXES, pairs)  9.13 us
    ppermute x11, starting transfers between devices, swap_cores(): return lax.ppermute(value, AXES, pairs)  2.45 us
    pallas_call x2, Pallas kernels, early(): call(bind(early_kernel), [v_shape, u_shape, v2_shape], 0, 6, [vm(X, S + H...  2.32 us
    ppermute x2, starting transfers between devices, swap_sides(): return lax.ppermute(value, AXES, pairs)  2.19 us
    pallas_call x1, Pallas kernels, slab_shards(): call(bind(last_kernel), [v_shape, u_shape, v2_shape, f32(2 * Pn * (3 * S...  2.09 us
    ppermute x2, starting transfers between devices, swap_odd(): return lax.ppermute(value, AXES, pairs)  2.06 us
    pallas_call x1, Pallas kernels, slab_shards(): call(bind(first_kernel), [wide, v_shape, v2_shape, slab, f32(1, LANES)],...  1.89 us
  transfers between devices with their start and end apart: 17, of which 8 were waited for; matrix products, arithmetic and copies ran while one was open for 0% of the time, Pallas kernels for 10%

profile of v3, /device:TPU:0, one launch (start us, length us, event | category | flops | bytes accessed | tf_op | source)
XLA Modules:
  0.0 72.5 jit_solution(8159292985452552771)
XLA Ops:
  0.6 0.6 collective-permute-start
  1.2 0.1 collective-permute-start.1
  1.3 1.2 %shard_map.59 = (f32[2,128,128]{2,1,0:T(8,128)S(1)}, f32[1,128]{1,0:T(1,128)S(1)}) custom-call(f32[8,32,128]{2,1,0:T(8,128)} %src_hbm.1, f32[8,32,128]{2,1,0:T(8,128)} %tgt_hbm.1), custom_call_target="tpu_custom_call" | custom-call | tf_op jit(solution)/shard_map/pallas_call | solution.py:745
  2.5 0.0 collective-permute-done.src_ref
  2.5 0.3 collective-permute-done.1.tgt_ref
  2.7 0.1 shard_map.60
  2.9 18.4 %all_to_all.10 = f32[528,1,128]{2,1,0:T(1,128)S(1)} all-to-all(f32[528,1,128]{2,1,0:T(1,128)S(1)} %bitcast.13), channel_id=1, replica_groups=mesh['gx'=4,'gy'=4,'gz'=2] {'gx','gy'}, dimensions={0} | all-to-all | bytes 540672 | tf_op jit(solution)/shard_map/all_to_all | solution.py:162
  21.2 0.2 shard_map.63.own
  21.4 0.0 copy-start
  21.4 0.0 copy-start.1
  21.4 1.0 %collective-permute-start.5 = (f32[17,16,128]{2,1,0:T(8,128)S(1)}, f32[17,16,128]{2,1,0:T(8,128)S(1)}, u32[]{:S(2)}, u32[]{:S(2)}) collective-permute-start(f32[17,16,128]{2,1,0:T(8,128)S(1)} %shard_map.63.own), channel_id=1, source_target_pairs={{0,4},{1,5},{8,16},{9,17},{16,8},{17,9},{24,26},{25,27},{26,24},{2... | collective-permute-start | bytes 417800 | tf_op jit(solution)/shard_map/ppermute | solution.py:151
  22.4 0.3 collective-permute-start.4
  22.7 0.2 shard_map.61.own
  22.8 0.1 collective-permute-start.6
  22.9 1.1 %collective-permute-start.3 = (f32[16,16,128]{2,1,0:T(8,128)S(1)}, f32[16,16,128]{2,1,0:T(8,128)S(1)}, u32[]{:S(2)}, u32[]{:S(2)}) collective-permute-start(f32[16,16,128]{2,1,0:T(8,128)S(1)} %shard_map.61.own), channel_id=1, source_target_pairs={{0,4},{1,5},{8,16},{9,17},{16,8},{17,9},{24,26},{25,27},{26,24},{2... | collective-permute-start | bytes 393224 | tf_op jit(solution)/shard_map/ppermute | solution.py:151
  24.0 1.2 %collective-permute-start.2 = (f32[16,16,128]{2,1,0:T(8,128)S(1)}, f32[16,16,128]{2,1,0:T(8,128)S(1)}, u32[]{:S(2)}, u32[]{:S(2)}) collective-permute-start(f32[16,16,128]{2,1,0:T(8,128)S(1)} %shard_map.61.own), channel_id=1, source_target_pairs={{0,8},{1,9},{8,0},{9,1},{16,24},{17,25},{24,16},{25,17},{26,18},{2... | collective-permute-start | bytes 393224 | tf_op jit(solution)/shard_map/ppermute | solution.py:142
  25.2 0.0 collective-permute-done.6.own2
  25.2 0.0 collective-permute-start.7
  25.2 1.8 %collective-permute-done.5.odd = f32[17,16,128]{2,1,0:T(8,128)S(1)} collective-permute-done((f32[17,16,128]{2,1,0:T(8,128)S(1)}, f32[17,16,128]{2,1,0:T(8,128)S(1)}, u32[]{:S(2)}, u32[]{:S(2)}) %collective-permute-start.5) | collective-permute-done | bytes 139296 | tf_op jit(solution)/shard_map/ppermute | solution.py:151
  27.1 1.1 %collective-permute-done.4.even = f32[17,16,128]{2,1,0:T(8,128)S(1)} collective-permute-done((f32[17,16,128]{2,1,0:T(8,128)S(1)}, f32[17,16,128]{2,1,0:T(8,128)S(1)}, u32[]{:S(2)}, u32[]{:S(2)}) %collective-permute-start.4) | collective-permute-done | bytes 139296 | tf_op jit(solution)/shard_map/ppermute | solution.py:142
  28.2 0.0 collective-permute-start.8
  28.2 0.5 collective-permute-start.9
  28.7 0.0 copy-done
  28.7 0.0 copy-done.1
  28.7 0.8 %shard_map.62 = (f32[14,8,128]{2,1,0:T(8,128)S(1)}, bf16[256,256]{1,0:T(8,128)(2,1)S(1)}, bf16[256,256]{1,0:T(8,128)(2,1)S(1)}, bf16[256,256]{1,0:T(8,128)(2,1)S...) custom-call(f32[5]{0:T(128)S(1)} %copy-done, ...), custom_call_target="tpu_custom_call" | custom-call | tf_op jit(solution)/shard_map/pallas_call | solution.py:758
  29.5 0.0 collective-permute-done.3.odd
  29.6 0.7 %collective-permute-done.2.even = f32[16,16,128]{2,1,0:T(8,128)S(1)} collective-permute-done((f32[16,16,128]{2,1,0:T(8,128)S(1)}, f32[16,16,128]{2,1,0:T(8,128)S(1)}, u32[]{:S(2)}, u32[]{:S(2)}) %collective-permute-start.2) | collective-permute-done | bytes 131104 | tf_op jit(solution)/shard_map/ppermute | solution.py:142
  30.3 0.0 collective-permute-start.10
  30.3 0.5 collective-permute-start.11
  30.8 0.8 %collective-permute-done.10.even2 = f32[16,16,128]{2,1,0:T(8,128)S(1)} collective-permute-done((f32[16,16,128]{2,1,0:T(8,128)S(1)}, f32[16,16,128]{2,1,0:T(8,128)S(1)}, u32[]{:S(2)}, u32[]{:S(2)}) %collective-permute-start.10) | collective-permute-done | bytes 131104 | tf_op jit(solution)/shard_map/ppermute | solution.py:137
  31.6 0.2 collective-permute-done.11.odd2
  31.8 1.0 %shard_map.64 = (f32[32,48,128]{2,1,0:T(8,128)S(1)}, f32[32,40,128]{2,1,0:T(8,128)S(1)}) custom-call(f32[14,8,128]{2,1,0:T(8,128)S(1)} %get-tuple-element.47.taps_ref, bf16[256,256]{1,0:T(8,128)(2,1)S(1)} %get-tuple-element.48.quad_ref, f32[48,128]{1,0:T(8,128)S(1)} %get-tuple-element.53.plane_ref, f32[32,128]{1,0:T(8,128)S(1)} %get-tuple-element.54.line_ref, ...), custom_call_target="tpu_custom_call" | custom-call | tf_op jit(solution)/shard_map/pallas_call | solution.py:776
  32.8 0.0 collective-permute-done.7.own2
  32.8 0.0 collective-permute-done.8.even2
  32.8 0.0 collective-permute-done.9.odd2
  32.9 1.9 %shard_map.65 = (f32[32,48,128]{2,1,0:T(8,128)S(1)}, f32[32,40,128]{2,1,0:T(8,128)S(1)}, f32[32,24,128]{2,1,0:T(8,128)S(1)}, f32[32,16,128]{2,1,0:T(8,128)S(1)}, f32[1,128]{1,0:T(1,128)S(1)}) custom-call(f32[14,8,128]{2,1,0:T(8,128)S(1)} %get-tuple-element.47.taps_ref, bf16[256,256]{1,0:T(8,128)(2,1)S(1)} %get-tuple-element.48.quad_ref, ...), custom_call_target="tpu_custom_call" | custom-call | tf_op jit(solution)/shard_map/pallas_call | solution.py:779
  34.8 1.1 %collective-permute-start.12 = (f32[32,16,128]{2,1,0:T(8,128)S(1)}, f32[32,16,128]{2,1,0:T(8,128)S(1)}, u32[]{:S(2)}, u32[]{:S(2)}) collective-permute-start(f32[32,16,128]{2,1,0:T(8,128)S(1)} %get-tuple-element.60.mine), channel_id=1, source_target_pairs={{0,5},{8,1},{16,9},{24,17},{26,25},{18,27},{10,19},{2,11},{6,3},{1... | collective-permute-start | bytes 786440 | tf_op jit(solution)/shard_map/ppermute | solution.py:157
  35.9 4.8 %collective-permute-done.12.side = f32[32,16,128]{2,1,0:T(8,128)S(1)} collective-permute-done((f32[32,16,128]{2,1,0:T(8,128)S(1)}, f32[32,16,128]{2,1,0:T(8,128)S(1)}, u32[]{:S(2)}, u32[]{:S(2)}) %collective-permute-start.12) | collective-permute-done | bytes 262176 | tf_op jit(solution)/shard_map/ppermute | solution.py:157
  40.6 0.3 collective-permute-start.13
  40.9 1.2 %shard_map.66 = (f32[32,40,128]{2,1,0:T(8,128)S(1)}, f32[32,32,128]{2,1,0:T(8,128)S(1)}, f32[32,24,128]{2,1,0:T(8,128)S(1)}) custom-call(f32[14,8,128]{2,1,0:T(8,128)S(1)} %get-tuple-element.47.taps_ref, bf16[256,256]{1,0:T(8,128)(2,1)S(1)} %get-tuple-element.48.quad_ref, f32[32,16,128]{2,1,0:T(8,128)S(1)} %get-tuple-element.60.mine, ...), custom_call_target="tpu_custom_call" | custom-call | tf_op jit(solution)/shard_map/pallas_call | solution.py:785
  42.1 0.0 collective-permute-done.13.other
  42.2 1.6 %shard_map.67 = (f32[32,40,128]{2,1,0:T(8,128)S(1)}, f32[32,32,128]{2,1,0:T(8,128)S(1)}, f32[32,24,128]{2,1,0:T(8,128)S(1)}, f32[32,16,128]{2,1,0:T(8,128)S(1)}) custom-call(f32[14,8,128]{2,1,0:T(8,128)S(1)} %get-tuple-element.47.taps_ref, ...), custom_call_target="tpu_custom_call", output_to_operand_aliasing={{0}: (6, {}), {1}: (7, {}), {2}: (8, {})} | custom-call | tf_op jit(solution)/shard_map/pallas_call | solution.py:794
  43.7 1.1 %collective-permute-start.14 = (f32[32,16,128]{2,1,0:T(8,128)S(1)}, f32[32,16,128]{2,1,0:T(8,128)S(1)}, u32[]{:S(2)}, u32[]{:S(2)}) collective-permute-start(f32[32,16,128]{2,1,0:T(8,128)S(1)} %get-tuple-element.65.mine), channel_id=1, source_target_pairs={{0,5},{8,1},{16,9},{24,17},{26,25},{18,27},{10,19},{2,11},{6,3},{1... | collective-permute-start | bytes 786440 | tf_op jit(solution)/shard_map/ppermute | solution.py:157
  44.8 0.4 shard_map.68.gaps
  45.2 4.4 %collective-permute-done.14.side = f32[32,16,128]{2,1,0:T(8,128)S(1)} collective-permute-done((f32[32,16,128]{2,1,0:T(8,128)S(1)}, f32[32,16,128]{2,1,0:T(8,128)S(1)}, u32[]{:S(2)}, u32[]{:S(2)}) %collective-permute-start.14) | collective-permute-done | bytes 262176 | tf_op jit(solution)/shard_map/ppermute | solution.py:157
  49.6 0.3 collective-permute-start.15
  49.9 1.2 %shard_map.69 = (f32[32,40,128]{2,1,0:T(8,128)S(1)}, f32[32,32,128]{2,1,0:T(8,128)S(1)}, f32[32,24,128]{2,1,0:T(8,128)S(1)}) custom-call(f32[14,8,128]{2,1,0:T(8,128)S(1)} %get-tuple-element.47.taps_ref, bf16[256,256]{1,0:T(8,128)(2,1)S(1)} %get-tuple-element.48.quad_ref, f32[32,16,128]{2,1,0:T(8,128)S(1)} %get-tuple-element.65.mine, ...), custom_call_target="tpu_custom_call" | custom-call | tf_op jit(solution)/shard_map/pallas_call | solution.py:785
  51.1 0.0 collective-permute-done.15.other
  51.1 2.1 %shard_map.70 = (f32[32,40,128]{2,1,0:T(8,128)S(1)}, f32[32,32,128]{2,1,0:T(8,128)S(1)}, f32[32,24,128]{2,1,0:T(8,128)S(1)}, f32[800,128]{1,0:T(8,128)S(1)}) custom-call(f32[14,8,128]{2,1,0:T(8,128)S(1)} %get-tuple-element.47.taps_ref, ...), custom_call_target="tpu_custom_call", output_to_operand_aliasing={{0}: (11, {}), {1}: (12, {}), {2}: (13, {})} | custom-call | tf_op jit(solution)/shard_map/pallas_call | solution.py:803
  53.2 16.5 %all_to_all.11 = f32[800,1,128]{2,1,0:T(1,128)S(1)} all-to-all(f32[800,1,128]{2,1,0:T(1,128)S(1)} %bitcast.14), channel_id=1, replica_groups=mesh['gx'=4,'gy'=4,'gz'=2] {'gx','gy','gz'}, dimensions={0} | all-to-all | bytes 819200 | tf_op jit(solution)/shard_map/all_to_all | solution.py:162
  69.7 0.4 shard_map.71
  70.1 0.1 collective-permute-start.16
  70.2 1.6 %shard_map.72 = (f32[6]{0:T(128)}, f32[3,8,32,128]{3,2,1,0:T(8,128)}) custom-call(bf16[256,256]{1,0:T(8,128)(2,1)S(1)} %get-tuple-element.44.high_ref, bf16[256,256]{1,0:T(8,128)(2,1)S(1)} %get-tuple-element.45.low_ref, bf16[256,384]{1,0:T(8,128)(2,1)S(1)} %get-tuple-element.78.d_high, bf16[256,384]{1,0:T(8,128)(2,1)S(1)} %get-tuple-element.79.d_low, ...), custom_call_target="tpu_custom_call" | custom-call | tf_op jit(solution)/shard_map/pallas_call | solution.py:816
  71.7 0.0 collective-permute-done.16.recv_ref
  71.7 0.7 shard_map.73
Async XLA Ops:
  0.6 1.8 %collective-permute-start = (f32[8,32,128]{2,1,0:T(8,128)}, f32[8,32,128]{2,1,0:T(8,128)S(1)}, u32[]{:S(2)}, u32[]{:S(2)}) collective-permute-start(f32[8,32,128]{2,1,0:T(8,128)} %src_hbm.1), channel_id=1, source_target_pairs={{0,1},{1,0},{8,9},{9,8},{16,17},{17,16},{24,25},{25,24},{26,27},{2... | collective-permute-start | bytes 393224 | tf_op jit(solution)/shard_map/ppermute | solution.py:137
  1.2 1.6 %collective-permute-start.1 = (f32[8,32,128]{2,1,0:T(8,128)}, f32[8,32,128]{2,1,0:T(8,128)S(1)}, u32[]{:S(2)}, u32[]{:S(2)}) collective-permute-start(f32[8,32,128]{2,1,0:T(8,128)} %tgt_hbm.1), channel_id=1, source_target_pairs={{0,1},{1,0},{8,9},{9,8},{16,17},{17,16},{24,25},{25,24},{26,27},{2... | collective-permute-start | bytes 393224 | tf_op jit(solution)/shard_map/ppermute | solution.py:137
  21.4 7.3 %copy-start = (f32[5]{0:T(128)S(1)}, f32[5]{0:T(128)}, u32[]{:S(2)}) copy-start(f32[5]{0:T(128)} %k_ref.1) | copy-start | bytes 64
  21.4 7.3 %copy-start.1 = (f32[9]{0:T(128)S(1)}, f32[9]{0:T(128)}, u32[]{:S(2)}) copy-start(f32[9]{0:T(128)} %s_ref.1) | copy-start | bytes 112
  21.4 5.6 %collective-permute-start.5 = (f32[17,16,128]{2,1,0:T(8,128)S(1)}, f32[17,16,128]{2,1,0:T(8,128)S(1)}, u32[]{:S(2)}, u32[]{:S(2)}) collective-permute-start(f32[17,16,128]{2,1,0:T(8,128)S(1)} %shard_map.63.own), channel_id=1, source_target_pairs={{0,4},{1,5},{8,16},{9,17},{16,8},{17,9},{24,26},{25,27},{26,24},{2... | collective-permute-start | bytes 417800 | tf_op jit(solution)/shard_map/ppermute | solution.py:151
  22.4 5.8 %collective-permute-start.4 = (f32[17,16,128]{2,1,0:T(8,128)S(1)}, f32[17,16,128]{2,1,0:T(8,128)S(1)}, u32[]{:S(2)}, u32[]{:S(2)}) collective-permute-start(f32[17,16,128]{2,1,0:T(8,128)S(1)} %shard_map.63.own), channel_id=1, source_target_pairs={{0,8},{1,9},{8,0},{9,1},{16,24},{17,25},{24,16},{25,17},{26,18},{2... | collective-permute-start | bytes 417800 | tf_op jit(solution)/shard_map/ppermute | solution.py:142
  22.8 2.4 %collective-permute-start.6 = (f32[16,16,128]{2,1,0:T(8,128)S(1)}, f32[16,16,128]{2,1,0:T(8,128)S(1)}, u32[]{:S(2)}, u32[]{:S(2)}) collective-permute-start(f32[16,16,128]{2,1,0:T(8,128)S(1)} %shard_map.61.own), channel_id=1, source_target_pairs={{0,1},{1,0},{8,9},{9,8},{16,17},{17,16},{24,25},{25,24},{26,27},{2... | collective-permute-start | bytes 393224 | tf_op jit(solution)/shard_map/ppermute | solution.py:137
  22.9 6.6 %collective-permute-start.3 = (f32[16,16,128]{2,1,0:T(8,128)S(1)}, f32[16,16,128]{2,1,0:T(8,128)S(1)}, u32[]{:S(2)}, u32[]{:S(2)}) collective-permute-start(f32[16,16,128]{2,1,0:T(8,128)S(1)} %shard_map.61.own), channel_id=1, source_target_pairs={{0,4},{1,5},{8,16},{9,17},{16,8},{17,9},{24,26},{25,27},{26,24},{2... | collective-permute-start | bytes 393224 | tf_op jit(solution)/shard_map/ppermute | solution.py:151
  24.0 6.3 %collective-permute-start.2 = (f32[16,16,128]{2,1,0:T(8,128)S(1)}, f32[16,16,128]{2,1,0:T(8,128)S(1)}, u32[]{:S(2)}, u32[]{:S(2)}) collective-permute-start(f32[16,16,128]{2,1,0:T(8,128)S(1)} %shard_map.61.own), channel_id=1, source_target_pairs={{0,8},{1,9},{8,0},{9,1},{16,24},{17,25},{24,16},{25,17},{26,18},{2... | collective-permute-start | bytes 393224 | tf_op jit(solution)/shard_map/ppermute | solution.py:142
  25.2 7.6 %collective-permute-start.7 = (f32[17,16,128]{2,1,0:T(8,128)S(1)}, f32[17,16,128]{2,1,0:T(8,128)S(1)}, u32[]{:S(2)}, u32[]{:S(2)}) collective-permute-start(f32[17,16,128]{2,1,0:T(8,128)S(1)} %shard_map.63.own), channel_id=1, source_target_pairs={{0,1},{1,0},{8,9},{9,8},{16,17},{17,16},{24,25},{25,24},{26,27},{2... | collective-permute-start | bytes 417800 | tf_op jit(solution)/shard_map/ppermute | solution.py:137
  28.2 4.6 %collective-permute-start.8 = (f32[17,16,128]{2,1,0:T(8,128)S(1)}, f32[17,16,128]{2,1,0:T(8,128)S(1)}, u32[]{:S(2)}, u32[]{:S(2)}) collective-permute-start(f32[17,16,128]{2,1,0:T(8,128)S(1)} %collective-permute-done.4.even), channel_id=1, source_target_pairs={{0,1},{1,0},{8,9},{9,8},{16,17},{17,16},{24,25},{25,24},{26,27},{2... | collective-permute-start | bytes 417800 | tf_op jit(solution)/shard_map/ppermute | solution.py:137
  28.2 4.7 %collective-permute-start.9 = (f32[17,16,128]{2,1,0:T(8,128)S(1)}, f32[17,16,128]{2,1,0:T(8,128)S(1)}, u32[]{:S(2)}, u32[]{:S(2)}) collective-permute-start(f32[17,16,128]{2,1,0:T(8,128)S(1)} %collective-permute-done.5.odd), channel_id=1, source_target_pairs={{0,1},{1,0},{8,9},{9,8},{16,17},{17,16},{24,25},{25,24},{26,27},{2... | collective-permute-start | bytes 417800 | tf_op jit(solution)/shard_map/ppermute | solution.py:137
  30.3 1.3 %collective-permute-start.10 = (f32[16,16,128]{2,1,0:T(8,128)S(1)}, f32[16,16,128]{2,1,0:T(8,128)S(1)}, u32[]{:S(2)}, u32[]{:S(2)}) collective-permute-start(f32[16,16,128]{2,1,0:T(8,128)S(1)} %collective-permute-done.2.even), channel_id=1, source_target_pairs={{0,1},{1,0},{8,9},{9,8},{16,17},{17,16},{24,25},{25,24},{26,27},{2... | collective-permute-start | bytes 393224 | tf_op jit(solution)/shard_map/ppermute | solution.py:137
  30.3 1.5 %collective-permute-start.11 = (f32[16,16,128]{2,1,0:T(8,128)S(1)}, f32[16,16,128]{2,1,0:T(8,128)S(1)}, u32[]{:S(2)}, u32[]{:S(2)}) collective-permute-start(f32[16,16,128]{2,1,0:T(8,128)S(1)} %collective-permute-done.3.odd), channel_id=1, source_target_pairs={{0,1},{1,0},{8,9},{9,8},{16,17},{17,16},{24,25},{25,24},{26,27},{2... | collective-permute-start | bytes 393224 | tf_op jit(solution)/shard_map/ppermute | solution.py:137
  34.8 5.9 %collective-permute-start.12 = (f32[32,16,128]{2,1,0:T(8,128)S(1)}, f32[32,16,128]{2,1,0:T(8,128)S(1)}, u32[]{:S(2)}, u32[]{:S(2)}) collective-permute-start(f32[32,16,128]{2,1,0:T(8,128)S(1)} %get-tuple-element.60.mine), channel_id=1, source_target_pairs={{0,5},{8,1},{16,9},{24,17},{26,25},{18,27},{10,19},{2,11},{6,3},{1... | collective-permute-start | bytes 786440 | tf_op jit(solution)/shard_map/ppermute | solution.py:157
  40.6 1.5 %collective-permute-start.13 = (f32[32,16,128]{2,1,0:T(8,128)S(1)}, f32[32,16,128]{2,1,0:T(8,128)S(1)}, u32[]{:S(2)}, u32[]{:S(2)}) collective-permute-start(f32[32,16,128]{2,1,0:T(8,128)S(1)} %collective-permute-done.12.side), channel_id=1, source_target_pairs={{0,1},{1,0},{8,9},{9,8},{16,17},{17,16},{24,25},{25,24},{26,27},{2... | collective-permute-start | bytes 786440 | tf_op jit(solution)/shard_map/ppermute | solution.py:137
  43.7 5.9 %collective-permute-start.14 = (f32[32,16,128]{2,1,0:T(8,128)S(1)}, f32[32,16,128]{2,1,0:T(8,128)S(1)}, u32[]{:S(2)}, u32[]{:S(2)}) collective-permute-start(f32[32,16,128]{2,1,0:T(8,128)S(1)} %get-tuple-element.65.mine), channel_id=1, source_target_pairs={{0,5},{8,1},{16,9},{24,17},{26,25},{18,27},{10,19},{2,11},{6,3},{1... | collective-permute-start | bytes 786440 | tf_op jit(solution)/shard_map/ppermute | solution.py:157
  49.6 1.5 %collective-permute-start.15 = (f32[32,16,128]{2,1,0:T(8,128)S(1)}, f32[32,16,128]{2,1,0:T(8,128)S(1)}, u32[]{:S(2)}, u32[]{:S(2)}) collective-permute-start(f32[32,16,128]{2,1,0:T(8,128)S(1)} %collective-permute-done.14.side), channel_id=1, source_target_pairs={{0,1},{1,0},{8,9},{9,8},{16,17},{17,16},{24,25},{25,24},{26,27},{2... | collective-permute-start | bytes 786440 | tf_op jit(solution)/shard_map/ppermute | solution.py:137
  70.1 1.7 %collective-permute-start.16 = (f32[3,4,32,128]{3,2,1,0:T(8,128)S(1)}, f32[3,4,32,128]{3,2,1,0:T(8,128)S(1)}, u32[]{:S(2)}, u32[]{:S(2)}) collective-permute-start(f32[3,4,32,128]{3,2,1,0:T(8,128)S(1)} %bitcast.15), channel_id=1, source_target_pairs={{0,1},{1,0},{8,9},{9,8},{16,17},{17,16},{24,25},{25,24},{26,27},{2... | collective-permute-start | bytes 589832 | tf_op jit(solution)/shard_map/ppermute | solution.py:137

commit v4 on v3

--- a/solution.py
+++ b/solution.py
@@ -519,11 +519,8 @@
     rows = S + 2 * H - 2 * R
     mask = inside(plan, at, R, rows)
 
-    def v_step(x, carry):
+    for x in range(X):
         v[x] = jnp.where(mask, tw[x, R : R + rows, :] / ku[x], 0.0)
-        return carry
-
-    lax.fori_loop(0, X, v_step, 0, unroll=4)
     step = functools.partial(scale_step, plan, at, taps, quad_ref)
     run_passes(plan, [
         step(zb, v, 0, u, sw, 2 * R, 0, rows - 2 * R),
@@ -705,7 +702,7 @@
     smooth_z(1 - lax.axis_index("gz"), high_ref, low_ref, d_high, d_low, emit)
 
 
-def home_kernel(plan, high_ref, low_ref, d_high, d_low, in_ref, mis_ref, out_hbm, keep, sems):
+def home_kernel(plan, high_ref, low_ref, d_high, d_low, in_ref, mis_hbm, out_hbm, keep, mis_ref, sems):
     c = lax.axis_index("gz")
     gs = plan.gs
     copies = [
@@ -721,6 +718,8 @@
     gone = sum_rows(in_ref, 3 * plan.S // 2 + 1) / plan.cells
     for t in range(ITERS):
         mis_ref[t] = jnp.sum(jnp.where(lane_at() == t, gone, 0.0))
+    copies.append(pltpu.make_async_copy(mis_ref, mis_hbm, sems.at[3]))
+    copies[-1].start()
     for copy in copies:
         copy.wait()
 
@@ -814,8 +813,8 @@
     recv = swap_cores(plan, send.reshape(half))
     whole = f32(3, plan.bx, plan.by, LANES)
     mismatch, displacement = call(
-        bind(home_kernel), [f32(ITERS), whole], 0, 5, [vm(*half), pltpu.SemaphoreType.DMA((3,))],
-        smem_out=1, any_out=1,
+        bind(home_kernel), [f32(ITERS), whole], 0, 5, [vm(*half), pltpu.SMEM((ITERS,), jnp.float32), pltpu.SemaphoreType.DMA((4,))],
+        any_out=2,
     )(high, low, *splits, spread)
     (displacement,) = call(
         bind(place_kernel), [whole], 0, 1, [pltpu.SemaphoreType.DMA((3,))], n_any=1, any_out=1,

time: 72.7 us -> 72.5 us (level)
  transfers between devices with their start and end apart: 17 -> 17, of which waited for: 8 -> 9; matrix products, arithmetic and copies ran while one was open for 0% -> 0% of each run, Pallas kernels for 10% -> 10%
where the time goes in v4:
time: 72.5 us; the launch traced here: 72.3 us
  blocking collectives  34.8 us (48%)
  waiting for transfers between devices  14.6 us (20%)
  Pallas kernels  13.9 us (19%)
  starting transfers between devices  8.21 us (11%)
  between operations  0.82 us (1%)
    all_to_all x2, blocking collectives, trade_chunks(): out = lax.all_to_all(value.reshape(rows, 1, lanes), axes, 0, 0, tiled=True)  34.8 us
    ppermute x2, waiting for transfers between devices, swap_sides(): return lax.ppermute(value, AXES, pairs)  9.13 us
    ppermute x11, starting transfers between devices, swap_cores(): return lax.ppermute(value, AXES, pairs)  2.45 us
    pallas_call x2, Pallas kernels, early(): call(bind(early_kernel), [v_shape, u_shape, v2_shape], 0, 6, [vm(X, S + H...  2.32 us
    ppermute x2, starting transfers between devices, swap_sides(): return lax.ppermute(value, AXES, pairs)  2.2 us
    pallas_call x1, Pallas kernels, slab_shards(): call(bind(last_kernel), [v_shape, u_shape, v2_shape, f32(2 * Pn * (3 * S...  2.09 us
    ppermute x2, starting transfers between devices, swap_odd(): return lax.ppermute(value, AXES, pairs)  2.06 us
    pallas_call x1, Pallas kernels, slab_shards(): call(bind(first_kernel), [wide, v_shape, v2_shape, slab, f32(1, LANES)],...  1.91 us
  transfers between devices with their start and end apart: 17, of which 9 were waited for; matrix products, arithmetic and copies ran while one was open for 0% of the time, Pallas kernels for 10%

profile of v4, /device:TPU:0, one launch (start us, length us, event | category | flops | bytes accessed | tf_op | source)
XLA Modules:
  0.0 72.3 jit_solution(9925023082446219470)
XLA Ops:
  0.6 0.6 collective-permute-start
  1.2 0.1 collective-permute-start.1
  1.3 1.2 %shard_map.59 = (f32[2,128,128]{2,1,0:T(8,128)S(1)}, f32[1,128]{1,0:T(1,128)S(1)}) custom-call(f32[8,32,128]{2,1,0:T(8,128)} %src_hbm.1, f32[8,32,128]{2,1,0:T(8,128)} %tgt_hbm.1), custom_call_target="tpu_custom_call" | custom-call | tf_op jit(solution)/shard_map/pallas_call | solution.py:744
  2.5 0.0 collective-permute-done.src_ref
  2.5 0.3 collective-permute-done.1.tgt_ref
  2.7 0.1 shard_map.60
  2.9 18.4 %all_to_all.10 = f32[528,1,128]{2,1,0:T(1,128)S(1)} all-to-all(f32[528,1,128]{2,1,0:T(1,128)S(1)} %bitcast.13), channel_id=1, replica_groups=mesh['gx'=4,'gy'=4,'gz'=2] {'gx','gy'}, dimensions={0} | all-to-all | bytes 540672 | tf_op jit(solution)/shard_map/all_to_all | solution.py:162
  21.2 0.2 shard_map.63.own
  21.4 0.0 copy-start
  21.4 0.0 copy-start.1
  21.4 1.0 %collective-permute-start.5 = (f32[17,16,128]{2,1,0:T(8,128)S(1)}, f32[17,16,128]{2,1,0:T(8,128)S(1)}, u32[]{:S(2)}, u32[]{:S(2)}) collective-permute-start(f32[17,16,128]{2,1,0:T(8,128)S(1)} %shard_map.63.own), channel_id=1, source_target_pairs={{0,4},{1,5},{8,16},{9,17},{16,8},{17,9},{24,26},{25,27},{26,24},{2... | collective-permute-start | bytes 417800 | tf_op jit(solution)/shard_map/ppermute | solution.py:151
  22.4 0.3 collective-permute-start.4
  22.7 0.2 shard_map.61.own
  22.8 0.1 collective-permute-start.6
  22.9 1.1 %collective-permute-start.3 = (f32[16,16,128]{2,1,0:T(8,128)S(1)}, f32[16,16,128]{2,1,0:T(8,128)S(1)}, u32[]{:S(2)}, u32[]{:S(2)}) collective-permute-start(f32[16,16,128]{2,1,0:T(8,128)S(1)} %shard_map.61.own), channel_id=1, source_target_pairs={{0,4},{1,5},{8,16},{9,17},{16,8},{17,9},{24,26},{25,27},{26,24},{2... | collective-permute-start | bytes 393224 | tf_op jit(solution)/shard_map/ppermute | solution.py:151
  24.0 1.2 %collective-permute-start.2 = (f32[16,16,128]{2,1,0:T(8,128)S(1)}, f32[16,16,128]{2,1,0:T(8,128)S(1)}, u32[]{:S(2)}, u32[]{:S(2)}) collective-permute-start(f32[16,16,128]{2,1,0:T(8,128)S(1)} %shard_map.61.own), channel_id=1, source_target_pairs={{0,8},{1,9},{8,0},{9,1},{16,24},{17,25},{24,16},{25,17},{26,18},{2... | collective-permute-start | bytes 393224 | tf_op jit(solution)/shard_map/ppermute | solution.py:142
  25.2 0.0 collective-permute-done.6.own2
  25.2 0.0 collective-permute-start.7
  25.2 1.8 %collective-permute-done.5.odd = f32[17,16,128]{2,1,0:T(8,128)S(1)} collective-permute-done((f32[17,16,128]{2,1,0:T(8,128)S(1)}, f32[17,16,128]{2,1,0:T(8,128)S(1)}, u32[]{:S(2)}, u32[]{:S(2)}) %collective-permute-start.5) | collective-permute-done | bytes 139296 | tf_op jit(solution)/shard_map/ppermute | solution.py:151
  27.1 1.1 %collective-permute-done.4.even = f32[17,16,128]{2,1,0:T(8,128)S(1)} collective-permute-done((f32[17,16,128]{2,1,0:T(8,128)S(1)}, f32[17,16,128]{2,1,0:T(8,128)S(1)}, u32[]{:S(2)}, u32[]{:S(2)}) %collective-permute-start.4) | collective-permute-done | bytes 139296 | tf_op jit(solution)/shard_map/ppermute | solution.py:142
  28.2 0.0 collective-permute-start.8
  28.2 0.5 collective-permute-start.9
  28.7 0.0 copy-done
  28.7 0.0 copy-done.1
  28.7 0.8 %shard_map.62 = (f32[14,8,128]{2,1,0:T(8,128)S(1)}, bf16[256,256]{1,0:T(8,128)(2,1)S(1)}, bf16[256,256]{1,0:T(8,128)(2,1)S(1)}, bf16[256,256]{1,0:T(8,128)(2,1)S...) custom-call(f32[5]{0:T(128)S(1)} %copy-done, ...), custom_call_target="tpu_custom_call" | custom-call | tf_op jit(solution)/shard_map/pallas_call | solution.py:757
  29.5 0.0 collective-permute-done.3.odd
  29.6 0.7 %collective-permute-done.2.even = f32[16,16,128]{2,1,0:T(8,128)S(1)} collective-permute-done((f32[16,16,128]{2,1,0:T(8,128)S(1)}, f32[16,16,128]{2,1,0:T(8,128)S(1)}, u32[]{:S(2)}, u32[]{:S(2)}) %collective-permute-start.2) | collective-permute-done | bytes 131104 | tf_op jit(solution)/shard_map/ppermute | solution.py:142
  30.3 0.0 collective-permute-start.10
  30.3 0.5 collective-permute-start.11
  30.8 0.8 %collective-permute-done.10.even2 = f32[16,16,128]{2,1,0:T(8,128)S(1)} collective-permute-done((f32[16,16,128]{2,1,0:T(8,128)S(1)}, f32[16,16,128]{2,1,0:T(8,128)S(1)}, u32[]{:S(2)}, u32[]{:S(2)}) %collective-permute-start.10) | collective-permute-done | bytes 131104 | tf_op jit(solution)/shard_map/ppermute | solution.py:137
  31.6 0.2 collective-permute-done.11.odd2
  31.8 1.0 %shard_map.64 = (f32[32,48,128]{2,1,0:T(8,128)S(1)}, f32[32,40,128]{2,1,0:T(8,128)S(1)}) custom-call(f32[14,8,128]{2,1,0:T(8,128)S(1)} %get-tuple-element.47.taps_ref, bf16[256,256]{1,0:T(8,128)(2,1)S(1)} %get-tuple-element.48.quad_ref, f32[48,128]{1,0:T(8,128)S(1)} %get-tuple-element.53.plane_ref, f32[32,128]{1,0:T(8,128)S(1)} %get-tuple-element.54.line_ref, ...), custom_call_target="tpu_custom_call" | custom-call | tf_op jit(solution)/shard_map/pallas_call | solution.py:775
  32.8 0.0 collective-permute-done.7.own2
  32.8 0.0 collective-permute-done.8.even2
  32.8 0.0 collective-permute-done.9.odd2
  32.9 1.9 %shard_map.65 = (f32[32,48,128]{2,1,0:T(8,128)S(1)}, f32[32,40,128]{2,1,0:T(8,128)S(1)}, f32[32,24,128]{2,1,0:T(8,128)S(1)}, f32[32,16,128]{2,1,0:T(8,128)S(1)}, f32[1,128]{1,0:T(1,128)S(1)}) custom-call(f32[14,8,128]{2,1,0:T(8,128)S(1)} %get-tuple-element.47.taps_ref, bf16[256,256]{1,0:T(8,128)(2,1)S(1)} %get-tuple-element.48.quad_ref, ...), custom_call_target="tpu_custom_call" | custom-call | tf_op jit(solution)/shard_map/pallas_call | solution.py:778
  34.8 1.1 %collective-permute-start.12 = (f32[32,16,128]{2,1,0:T(8,128)S(1)}, f32[32,16,128]{2,1,0:T(8,128)S(1)}, u32[]{:S(2)}, u32[]{:S(2)}) collective-permute-start(f32[32,16,128]{2,1,0:T(8,128)S(1)} %get-tuple-element.60.mine), channel_id=1, source_target_pairs={{0,5},{8,1},{16,9},{24,17},{26,25},{18,27},{10,19},{2,11},{6,3},{1... | collective-permute-start | bytes 786440 | tf_op jit(solution)/shard_map/ppermute | solution.py:157
  35.9 4.8 %collective-permute-done.12.side = f32[32,16,128]{2,1,0:T(8,128)S(1)} collective-permute-done((f32[32,16,128]{2,1,0:T(8,128)S(1)}, f32[32,16,128]{2,1,0:T(8,128)S(1)}, u32[]{:S(2)}, u32[]{:S(2)}) %collective-permute-start.12) | collective-permute-done | bytes 262176 | tf_op jit(solution)/shard_map/ppermute | solution.py:157
  40.6 0.3 collective-permute-start.13
  41.0 1.2 %shard_map.66 = (f32[32,40,128]{2,1,0:T(8,128)S(1)}, f32[32,32,128]{2,1,0:T(8,128)S(1)}, f32[32,24,128]{2,1,0:T(8,128)S(1)}) custom-call(f32[14,8,128]{2,1,0:T(8,128)S(1)} %get-tuple-element.47.taps_ref, bf16[256,256]{1,0:T(8,128)(2,1)S(1)} %get-tuple-element.48.quad_ref, f32[32,16,128]{2,1,0:T(8,128)S(1)} %get-tuple-element.60.mine, ...), custom_call_target="tpu_custom_call" | custom-call | tf_op jit(solution)/shard_map/pallas_call | solution.py:784
  42.1 0.0 collective-permute-done.13.other
  42.2 1.6 %shard_map.67 = (f32[32,40,128]{2,1,0:T(8,128)S(1)}, f32[32,32,128]{2,1,0:T(8,128)S(1)}, f32[32,24,128]{2,1,0:T(8,128)S(1)}, f32[32,16,128]{2,1,0:T(8,128)S(1)}) custom-call(f32[14,8,128]{2,1,0:T(8,128)S(1)} %get-tuple-element.47.taps_ref, ...), custom_call_target="tpu_custom_call", output_to_operand_aliasing={{0}: (6, {}), {1}: (7, {}), {2}: (8, {})} | custom-call | tf_op jit(solution)/shard_map/pallas_call | solution.py:793
  43.7 1.1 %collective-permute-start.14 = (f32[32,16,128]{2,1,0:T(8,128)S(1)}, f32[32,16,128]{2,1,0:T(8,128)S(1)}, u32[]{:S(2)}, u32[]{:S(2)}) collective-permute-start(f32[32,16,128]{2,1,0:T(8,128)S(1)} %get-tuple-element.65.mine), channel_id=1, source_target_pairs={{0,5},{8,1},{16,9},{24,17},{26,25},{18,27},{10,19},{2,11},{6,3},{1... | collective-permute-start | bytes 786440 | tf_op jit(solution)/shard_map/ppermute | solution.py:157
  44.8 0.4 shard_map.68.gaps
  45.2 4.4 %collective-permute-done.14.side = f32[32,16,128]{2,1,0:T(8,128)S(1)} collective-permute-done((f32[32,16,128]{2,1,0:T(8,128)S(1)}, f32[32,16,128]{2,1,0:T(8,128)S(1)}, u32[]{:S(2)}, u32[]{:S(2)}) %collective-permute-start.14) | collective-permute-done | bytes 262176 | tf_op jit(solution)/shard_map/ppermute | solution.py:157
  49.6 0.3 collective-permute-start.15
  49.9 1.2 %shard_map.69 = (f32[32,40,128]{2,1,0:T(8,128)S(1)}, f32[32,32,128]{2,1,0:T(8,128)S(1)}, f32[32,24,128]{2,1,0:T(8,128)S(1)}) custom-call(f32[14,8,128]{2,1,0:T(8,128)S(1)} %get-tuple-element.47.taps_ref, bf16[256,256]{1,0:T(8,128)(2,1)S(1)} %get-tuple-element.48.quad_ref, f32[32,16,128]{2,1,0:T(8,128)S(1)} %get-tuple-element.65.mine, ...), custom_call_target="tpu_custom_call" | custom-call | tf_op jit(solution)/shard_map/pallas_call | solution.py:784
  51.1 0.0 collective-permute-done.15.other
  51.1 2.1 %shard_map.70 = (f32[32,40,128]{2,1,0:T(8,128)S(1)}, f32[32,32,128]{2,1,0:T(8,128)S(1)}, f32[32,24,128]{2,1,0:T(8,128)S(1)}, f32[800,128]{1,0:T(8,128)S(1)}) custom-call(f32[14,8,128]{2,1,0:T(8,128)S(1)} %get-tuple-element.47.taps_ref, ...), custom_call_target="tpu_custom_call", output_to_operand_aliasing={{0}: (11, {}), {1}: (12, {}), {2}: (13, {})} | custom-call | tf_op jit(solution)/shard_map/pallas_call | solution.py:802
  53.2 16.5 %all_to_all.11 = f32[800,1,128]{2,1,0:T(1,128)S(1)} all-to-all(f32[800,1,128]{2,1,0:T(1,128)S(1)} %bitcast.14), channel_id=1, replica_groups=mesh['gx'=4,'gy'=4,'gz'=2] {'gx','gy','gz'}, dimensions={0} | all-to-all | bytes 819200 | tf_op jit(solution)/shard_map/all_to_all | solution.py:162
  69.7 0.4 shard_map.71
  70.1 0.1 collective-permute-start.16
  70.2 1.1 %shard_map.72 = (f32[6]{0:T(128)}, f32[3,8,32,128]{3,2,1,0:T(8,128)}) custom-call(bf16[256,256]{1,0:T(8,128)(2,1)S(1)} %get-tuple-element.44.high_ref, bf16[256,256]{1,0:T(8,128)(2,1)S(1)} %get-tuple-element.45.low_ref, bf16[256,384]{1,0:T(8,128)(2,1)S(1)} %get-tuple-element.78.d_high, bf16[256,384]{1,0:T(8,128)(2,1)S(1)} %get-tuple-element.79.d_low, ...), custom_call_target="tpu_custom_call" | custom-call | tf_op jit(solution)/shard_map/pallas_call | solution.py:815
  71.3 0.3 collective-permute-done.16.recv_ref
  71.6 0.7 shard_map.73
Async XLA Ops:
  0.6 1.8 %collective-permute-start = (f32[8,32,128]{2,1,0:T(8,128)}, f32[8,32,128]{2,1,0:T(8,128)S(1)}, u32[]{:S(2)}, u32[]{:S(2)}) collective-permute-start(f32[8,32,128]{2,1,0:T(8,128)} %src_hbm.1), channel_id=1, source_target_pairs={{0,1},{1,0},{8,9},{9,8},{16,17},{17,16},{24,25},{25,24},{26,27},{2... | collective-permute-start | bytes 393224 | tf_op jit(solution)/shard_map/ppermute | solution.py:137
  1.2 1.6 %collective-permute-start.1 = (f32[8,32,128]{2,1,0:T(8,128)}, f32[8,32,128]{2,1,0:T(8,128)S(1)}, u32[]{:S(2)}, u32[]{:S(2)}) collective-permute-start(f32[8,32,128]{2,1,0:T(8,128)} %tgt_hbm.1), channel_id=1, source_target_pairs={{0,1},{1,0},{8,9},{9,8},{16,17},{17,16},{24,25},{25,24},{26,27},{2... | collective-permute-start | bytes 393224 | tf_op jit(solution)/shard_map/ppermute | solution.py:137
  21.4 7.3 %copy-start = (f32[5]{0:T(128)S(1)}, f32[5]{0:T(128)}, u32[]{:S(2)}) copy-start(f32[5]{0:T(128)} %k_ref.1) | copy-start | bytes 64
  21.4 7.3 %copy-start.1 = (f32[9]{0:T(128)S(1)}, f32[9]{0:T(128)}, u32[]{:S(2)}) copy-start(f32[9]{0:T(128)} %s_ref.1) | copy-start | bytes 112
  21.4 5.6 %collective-permute-start.5 = (f32[17,16,128]{2,1,0:T(8,128)S(1)}, f32[17,16,128]{2,1,0:T(8,128)S(1)}, u32[]{:S(2)}, u32[]{:S(2)}) collective-permute-start(f32[17,16,128]{2,1,0:T(8,128)S(1)} %shard_map.63.own), channel_id=1, source_target_pairs={{0,4},{1,5},{8,16},{9,17},{16,8},{17,9},{24,26},{25,27},{26,24},{2... | collective-permute-start | bytes 417800 | tf_op jit(solution)/shard_map/ppermute | solution.py:151
  22.4 5.8 %collective-permute-start.4 = (f32[17,16,128]{2,1,0:T(8,128)S(1)}, f32[17,16,128]{2,1,0:T(8,128)S(1)}, u32[]{:S(2)}, u32[]{:S(2)}) collective-permute-start(f32[17,16,128]{2,1,0:T(8,128)S(1)} %shard_map.63.own), channel_id=1, source_target_pairs={{0,8},{1,9},{8,0},{9,1},{16,24},{17,25},{24,16},{25,17},{26,18},{2... | collective-permute-start | bytes 417800 | tf_op jit(solution)/shard_map/ppermute | solution.py:142
  22.8 2.4 %collective-permute-start.6 = (f32[16,16,128]{2,1,0:T(8,128)S(1)}, f32[16,16,128]{2,1,0:T(8,128)S(1)}, u32[]{:S(2)}, u32[]{:S(2)}) collective-permute-start(f32[16,16,128]{2,1,0:T(8,128)S(1)} %shard_map.61.own), channel_id=1, source_target_pairs={{0,1},{1,0},{8,9},{9,8},{16,17},{17,16},{24,25},{25,24},{26,27},{2... | collective-permute-start | bytes 393224 | tf_op jit(solution)/shard_map/ppermute | solution.py:137
  22.9 6.6 %collective-permute-start.3 = (f32[16,16,128]{2,1,0:T(8,128)S(1)}, f32[16,16,128]{2,1,0:T(8,128)S(1)}, u32[]{:S(2)}, u32[]{:S(2)}) collective-permute-start(f32[16,16,128]{2,1,0:T(8,128)S(1)} %shard_map.61.own), channel_id=1, source_target_pairs={{0,4},{1,5},{8,16},{9,17},{16,8},{17,9},{24,26},{25,27},{26,24},{2... | collective-permute-start | bytes 393224 | tf_op jit(solution)/shard_map/ppermute | solution.py:151
  24.0 6.3 %collective-permute-start.2 = (f32[16,16,128]{2,1,0:T(8,128)S(1)}, f32[16,16,128]{2,1,0:T(8,128)S(1)}, u32[]{:S(2)}, u32[]{:S(2)}) collective-permute-start(f32[16,16,128]{2,1,0:T(8,128)S(1)} %shard_map.61.own), channel_id=1, source_target_pairs={{0,8},{1,9},{8,0},{9,1},{16,24},{17,25},{24,16},{25,17},{26,18},{2... | collective-permute-start | bytes 393224 | tf_op jit(solution)/shard_map/ppermute | solution.py:142
  25.2 7.6 %collective-permute-start.7 = (f32[17,16,128]{2,1,0:T(8,128)S(1)}, f32[17,16,128]{2,1,0:T(8,128)S(1)}, u32[]{:S(2)}, u32[]{:S(2)}) collective-permute-start(f32[17,16,128]{2,1,0:T(8,128)S(1)} %shard_map.63.own), channel_id=1, source_target_pairs={{0,1},{1,0},{8,9},{9,8},{16,17},{17,16},{24,25},{25,24},{26,27},{2... | collective-permute-start | bytes 417800 | tf_op jit(solution)/shard_map/ppermute | solution.py:137
  28.2 4.6 %collective-permute-start.8 = (f32[17,16,128]{2,1,0:T(8,128)S(1)}, f32[17,16,128]{2,1,0:T(8,128)S(1)}, u32[]{:S(2)}, u32[]{:S(2)}) collective-permute-start(f32[17,16,128]{2,1,0:T(8,128)S(1)} %collective-permute-done.4.even), channel_id=1, source_target_pairs={{0,1},{1,0},{8,9},{9,8},{16,17},{17,16},{24,25},{25,24},{26,27},{2... | collective-permute-start | bytes 417800 | tf_op jit(solution)/shard_map/ppermute | solution.py:137
  28.2 4.7 %collective-permute-start.9 = (f32[17,16,128]{2,1,0:T(8,128)S(1)}, f32[17,16,128]{2,1,0:T(8,128)S(1)}, u32[]{:S(2)}, u32[]{:S(2)}) collective-permute-start(f32[17,16,128]{2,1,0:T(8,128)S(1)} %collective-permute-done.5.odd), channel_id=1, source_target_pairs={{0,1},{1,0},{8,9},{9,8},{16,17},{17,16},{24,25},{25,24},{26,27},{2... | collective-permute-start | bytes 417800 | tf_op jit(solution)/shard_map/ppermute | solution.py:137
  30.3 1.3 %collective-permute-start.10 = (f32[16,16,128]{2,1,0:T(8,128)S(1)}, f32[16,16,128]{2,1,0:T(8,128)S(1)}, u32[]{:S(2)}, u32[]{:S(2)}) collective-permute-start(f32[16,16,128]{2,1,0:T(8,128)S(1)} %collective-permute-done.2.even), channel_id=1, source_target_pairs={{0,1},{1,0},{8,9},{9,8},{16,17},{17,16},{24,25},{25,24},{26,27},{2... | collective-permute-start | bytes 393224 | tf_op jit(solution)/shard_map/ppermute | solution.py:137
  30.3 1.5 %collective-permute-start.11 = (f32[16,16,128]{2,1,0:T(8,128)S(1)}, f32[16,16,128]{2,1,0:T(8,128)S(1)}, u32[]{:S(2)}, u32[]{:S(2)}) collective-permute-start(f32[16,16,128]{2,1,0:T(8,128)S(1)} %collective-permute-done.3.odd), channel_id=1, source_target_pairs={{0,1},{1,0},{8,9},{9,8},{16,17},{17,16},{24,25},{25,24},{26,27},{2... | collective-permute-start | bytes 393224 | tf_op jit(solution)/shard_map/ppermute | solution.py:137
  34.8 5.9 %collective-permute-start.12 = (f32[32,16,128]{2,1,0:T(8,128)S(1)}, f32[32,16,128]{2,1,0:T(8,128)S(1)}, u32[]{:S(2)}, u32[]{:S(2)}) collective-permute-start(f32[32,16,128]{2,1,0:T(8,128)S(1)} %get-tuple-element.60.mine), channel_id=1, source_target_pairs={{0,5},{8,1},{16,9},{24,17},{26,25},{18,27},{10,19},{2,11},{6,3},{1... | collective-permute-start | bytes 786440 | tf_op jit(solution)/shard_map/ppermute | solution.py:157
  40.6 1.5 %collective-permute-start.13 = (f32[32,16,128]{2,1,0:T(8,128)S(1)}, f32[32,16,128]{2,1,0:T(8,128)S(1)}, u32[]{:S(2)}, u32[]{:S(2)}) collective-permute-start(f32[32,16,128]{2,1,0:T(8,128)S(1)} %collective-permute-done.12.side), channel_id=1, source_target_pairs={{0,1},{1,0},{8,9},{9,8},{16,17},{17,16},{24,25},{25,24},{26,27},{2... | collective-permute-start | bytes 786440 | tf_op jit(solution)/shard_map/ppermute | solution.py:137
  43.7 5.9 %collective-permute-start.14 = (f32[32,16,128]{2,1,0:T(8,128)S(1)}, f32[32,16,128]{2,1,0:T(8,128)S(1)}, u32[]{:S(2)}, u32[]{:S(2)}) collective-permute-start(f32[32,16,128]{2,1,0:T(8,128)S(1)} %get-tuple-element.65.mine), channel_id=1, source_target_pairs={{0,5},{8,1},{16,9},{24,17},{26,25},{18,27},{10,19},{2,11},{6,3},{1... | collective-permute-start | bytes 786440 | tf_op jit(solution)/shard_map/ppermute | solution.py:157
  49.6 1.5 %collective-permute-start.15 = (f32[32,16,128]{2,1,0:T(8,128)S(1)}, f32[32,16,128]{2,1,0:T(8,128)S(1)}, u32[]{:S(2)}, u32[]{:S(2)}) collective-permute-start(f32[32,16,128]{2,1,0:T(8,128)S(1)} %collective-permute-done.14.side), channel_id=1, source_target_pairs={{0,1},{1,0},{8,9},{9,8},{16,17},{17,16},{24,25},{25,24},{26,27},{2... | collective-permute-start | bytes 786440 | tf_op jit(solution)/shard_map/ppermute | solution.py:137
  70.1 1.5 %collective-permute-start.16 = (f32[3,4,32,128]{3,2,1,0:T(8,128)S(1)}, f32[3,4,32,128]{3,2,1,0:T(8,128)S(1)}, u32[]{:S(2)}, u32[]{:S(2)}) collective-permute-start(f32[3,4,32,128]{3,2,1,0:T(8,128)S(1)} %bitcast.15), channel_id=1, source_target_pairs={{0,1},{1,0},{8,9},{9,8},{16,17},{17,16},{24,25},{25,24},{26,27},{2... | collective-permute-start | bytes 589832 | tf_op jit(solution)/shard_map/ppermute | solution.py:137
